TPU v7x, 128 devices: a whole 4x4x4 slice. The times are simulated.
128 devices in a mesh: seq: 32 (over x, y, core), head: 4 (over z).
Axes of the slice: x: 4, y: 4, z: 4, core: 2. Of those that a mesh axis runs over, the one named last changes fastest.
Arguments:
- queries: bfloat16 [32768, 2048], P(('seq', 'head')), may hold values from -15 to 15
- key_rows: bfloat16 [32768, 2048], P(('seq', 'head')), may hold values from -15 to 15
- values: bfloat16 [32768, 2048], P(('seq', 'head')), may hold values from -6 to 6
- gate_logits: float32 [16], P('head'), may hold values from -1.5 to 1.5
- out_grad: bfloat16 [32768, 2048], P(('seq', 'head')), may hold values from -6 to 6
Outputs:
- output: bfloat16 [32768, 2048], P(('seq', 'head'))
- query_grad: bfloat16 [32768, 2048], P(('seq', 'head'))
- key_grad: bfloat16 [32768, 2048], P(('seq', 'head'))
- value_grad: bfloat16 [32768, 2048], P(('seq', 'head'))
All inputs are finite; a program needn't handle non-finite values.
Results may differ from a plain program's by a relative error of at most 0.0052.
The roundings to bfloat16 on the way count: a program that leaves them out, or rounds other values in their place, can miss the bound.
Values may be sent and summed in bfloat16 or wider, within the bound.
No kernel may reach another device: no remote copies, remote signals or barrier semaphores. Data moves between devices by JAX's collectives and lax.ppermute only.
A program may use at most 128 MiB of HBM per device.

v0:
```python
import functools

import jax
import jax.numpy as jnp
from jax import lax
from jax.experimental import pallas as pl
from jax.experimental.pallas import tpu as pltpu
from jax.sharding import PartitionSpec as P


DH = 128
HEADS = 4
HALF = 2 * DH
GROUP = HEADS * DH
ROWS = GROUP + 16 * HEADS
SHARE = 256
SEG = 4 * SHARE
SCALE = DH ** (-0.5)
LOG2E = 1.4426950408889634
f32 = jnp.float32
bf16 = jnp.bfloat16

HBM = pl.BlockSpec(memory_space=pltpu.HBM)
VMEM = pl.BlockSpec(memory_space=pltpu.VMEM)
SMEM = pl.BlockSpec(memory_space=pltpu.SMEM)


def shape(dims, dtype=bf16):
    return jax.ShapeDtypeStruct(dims, dtype)


def params(mib=56):
    return pltpu.CompilerParams(vmem_limit_bytes=mib << 20)


def cost(us):
    return pl.CostEstimate(flops=int(us * 5e8), bytes_accessed=int(us * 2e6), transcendentals=0)


def dot(a, b, ca, cb):
    return lax.dot_general(a, b, (((ca,), (cb,)), ((), ())), preferred_element_type=f32)


def feature(x):
    return jnp.where(x > 0, x + 1.0, jnp.exp(jnp.minimum(x, 0.0)))


def slope(x):
    return jnp.where(x > 0, jnp.ones_like(x), jnp.exp(jnp.minimum(x, 0.0)))


def split(x):
    high = x.astype(bf16)
    return high, (x - high.astype(f32)).astype(bf16)


def group_of(z, shift):
    return lax.rem(z + shift + 4, 4)


def run_copies(copies):
    for copy in copies:
        copy.start()
    for copy in copies:
        copy.wait()


def front_kernel(z_ref, k_ref, v_ref, q_ref, y_ref, *rest):
    partials, own_ref, firsts, seconds = rest[:3], rest[3], rest[4:7], rest[7:10]
    buf, sem_in, sem_out = rest[10:]
    z = z_ref[0]
    loads, stores = [], []
    for shift in (1, 2, 3):
        at = pl.multiple_of(group_of(z, shift) * GROUP, GROUP)
        for i, src in enumerate((k_ref, v_ref, q_ref, y_ref)):
            here = (shift - 1, i)
            for half, outs in enumerate((firsts, seconds)):
                cols = pl.ds(half * HALF, HALF)
                stores.append(
                    pltpu.make_async_copy(
                        buf.at[shift - 1, i, :, cols],
                        outs[shift - 1].at[i],
                        sem_out.at[shift - 1, i, half],
                    )
                )
            if i >= 2:
                copy = pltpu.make_async_copy(
                    src.at[:, pl.ds(at, GROUP)], buf.at[here], sem_in.at[shift - 1, i - 2]
                )
                copy.start()
                loads.append(copy)
            else:
                buf[here] = src[:, pl.ds(at, GROUP)]
                stores[-1].start()
                stores[-2].start()
    for shift in (1, 2, 3, 0):
        base = group_of(z, shift) * GROUP
        out = own_ref if shift == 0 else partials[shift - 1]
        for head in range(HEADS):
            cols = pl.ds(pl.multiple_of(base + head * DH, DH), DH)
            phi = feature(k_ref[:, cols].astype(f32)).astype(bf16)
            out[head * DH : (head + 1) * DH] = dot(phi, v_ref[:, cols], 0, 0).astype(out.dtype)
            sums = jnp.sum(phi.astype(f32), axis=0, keepdims=True)
            high = sums.astype(bf16).astype(f32)
            first = lax.broadcasted_iota(jnp.int32, (16, DH), 0) == 0
            rows = jnp.where(first, jnp.broadcast_to(high, (16, DH)), sums - high)
            out[GROUP + 16 * head : GROUP + 16 * head + 16] = rows.astype(out.dtype)
    for j, copy in enumerate(loads):
        copy.wait()
        at = 8 * (j // 2) + 2 * (2 + j % 2)
        stores[at].start()
        stores[at + 1].start()
    for copy in stores:
        copy.wait()


def front(z, k, v, q, y):
    out = pl.pallas_call(
        front_kernel,
        out_shape=[shape((ROWS, DH))] * 3
        + [shape((ROWS, DH), f32)]
        + [shape((4, SHARE, HALF))] * 6,
        in_specs=[SMEM, VMEM, VMEM, HBM, HBM],
        out_specs=[VMEM] * 4 + [HBM] * 6,
        scratch_shapes=[
            pltpu.VMEM((3, 4, SHARE, GROUP), bf16),
            pltpu.SemaphoreType.DMA((3, 2)),
            pltpu.SemaphoreType.DMA((3, 4, 2)),
        ],
        compiler_params=params(),
        cost_estimate=cost(6),
        name="front",
    )(z, k, v, q, y)
    return out[:3], out[3], out[4:7], out[7:10]


def update_kernel(own, r1, r2, r3, out_ref):
    for head in range(HEADS):
        rows = slice(head * DH, (head + 1) * DH)
        total = own[rows]
        for piece in (r1, r2, r3):
            total += piece[rows].astype(f32)
        out_ref[8 * head : 8 * head + 8, :16, :] = total.reshape(8, 16, DH)
        rows = slice(GROUP + 16 * head, GROUP + 16 * head + 16)
        sums = own[rows]
        for piece in (r1, r2, r3):
            sums += piece[rows].astype(f32)
        out_ref[8 * head, 16:24, :] = jnp.broadcast_to(sums[:1] + sums[1:2], (8, DH))


def update(own, received):
    return pl.pallas_call(
        update_kernel,
        out_shape=shape((32, 24, DH), f32),
        in_specs=[VMEM] * 4,
        out_specs=VMEM,
        compiler_params=params(),
        cost_estimate=cost(2),
        name="update",
    )(own, *received)


def scan_kernel(in_ref, out_ref, *, reverse):
    count = in_ref.shape[0]
    total = jnp.zeros(in_ref.shape[1:], f32)
    for step in range(count):
        at = count - 1 - step if reverse else step
        out_ref[at] = total.astype(out_ref.dtype)
        total += in_ref[at].astype(f32)


def scan(x, reverse):
    return pl.pallas_call(
        functools.partial(scan_kernel, reverse=reverse),
        out_shape=shape(x.shape, x.dtype),
        in_specs=[VMEM],
        out_specs=VMEM,
        compiler_params=params(),
        cost_estimate=cost(2),
        name="scan_later" if reverse else "scan_earlier",
    )(x)


def memory_of(mem_ref, head):
    at = pl.multiple_of(head * 8, 8)
    memory = mem_ref[pl.ds(at, 8), :16, :].reshape(DH, DH)
    high, low = split(memory)
    norm = mem_ref[at, 16:24, :][:1]
    return jnp.concatenate([high, low], 1), jnp.concatenate([high, low], 0), norm


def read_rows(memory, gate, q, y_low):
    right, _, norm = memory
    y = y_low.astype(f32)
    phi_low = feature(q).astype(bf16)
    phi = phi_low.astype(f32)
    both = dot(phi_low, right, 1, 0)
    raw = jnp.sum(phi * norm, 1, keepdims=True)
    inverse = 1.0 / jnp.maximum(raw, 1.0)
    retrieved = (both[:, :DH] + both[:, DH:]) * inverse
    denom_grad = jnp.where(
        raw > 1.0, -gate * jnp.sum(y * retrieved, 1, keepdims=True) * inverse, 0.0
    )
    return phi_low, phi, retrieved, denom_grad, gate * inverse


def results_of_rows(memory, gate, q, y_low, retrieved, denom_grad, weight, local, dq):
    _, below, norm = memory
    both = dot(y_low, below, 1, 1)
    back = (both[:, :DH] + both[:, DH:]) * weight + denom_grad * norm
    out = gate * retrieved + (1.0 - gate) * local
    return out.astype(bf16), (dq + back * slope(q)).astype(bf16)


def attention_kernel(
    z_ref, g_ref, k_ref, v_ref, q_ref, y_ref, r1, r2, r3, *refs, half
):
    refs = list(refs)
    mem_ref = refs.pop(0) if half else None
    if half:
        outs = [refs.pop(0) for _ in range(4)]
        local_ref, dq_ref, dkv_ref, sem_out = [refs.pop() for _ in range(4)]
    else:
        local_ref, dq_ref, dkv_ref = [refs.pop(0) for _ in range(3)]
    ks, vs, qs, ys, dks, dvs, sem = refs
    z = z_ref[0]
    own = pl.ds(pl.multiple_of(z * GROUP + half * HALF, HALF), HALF)
    copies = []
    for shift in range(4):
        rows = pl.ds(pl.multiple_of(group_of(z, -shift) * SHARE, SHARE), SHARE)
        for i, (src, dst) in enumerate(zip((k_ref, v_ref, q_ref, y_ref), (ks, vs, qs, ys))):
            block = src.at[:, own] if shift == 0 else (r1, r2, r3)[shift - 1].at[i]
            copies.append(pltpu.make_async_copy(block, dst.at[rows], sem.at[shift, i]))
    run_copies(copies)

    block = 512

    def one_head(head, carry):
        cs = pl.ds(pl.multiple_of(head * DH, DH), DH)
        rest = 1.0 - g_ref[2 * half + head]
        for i in range(SEG // block):
            rows = slice(i * block, (i + 1) * block)
            last = (i + 1) * block
            old = last - block
            q, y = qs[rows, cs], ys[rows, cs]
            k, v = ks[:last, cs], vs[:last, cs]
            scores = dot(q, k, 1, 1)
            below = lax.broadcasted_iota(jnp.int32, (block, block), 0) >= lax.broadcasted_iota(
                jnp.int32, (block, block), 1
            )
            diagonal = jnp.where(below, scores[:, old:], -jnp.inf)
            scores = jnp.concatenate([scores[:, :old], diagonal], 1) if i else diagonal
            top = jnp.max(scores, 1, keepdims=True)
            powers = jnp.exp2((scores - top) * (SCALE * LOG2E))
            prob = powers * (1.0 / jnp.sum(powers, 1, keepdims=True))
            low = prob.astype(bf16)
            dprob = dot(y, v, 1, 1) * rest
            mean = jnp.sum(prob * dprob, 1, keepdims=True)
            dlow = (prob * (dprob - mean)).astype(bf16)
            local_ref[rows, cs] = dot(low, v, 1, 0)
            dq_ref[rows, cs] = dot(dlow, k, 1, 0) * SCALE
            dv, dk = dot(y, low, 0, 0), dot(q, dlow, 0, 0)
            if i:
                dvs[:, :old] += dv[:, :old]
                dks[:, :old] += dk[:, :old]
            dvs[:, old:last] = dv[:, old:]
            dks[:, old:last] = dk[:, old:]
        dkv_ref[0, :, cs] = (dks[...].T * SCALE).astype(bf16)
        dkv_ref[1, :, cs] = (dvs[...].T * rest).astype(bf16)
        if half:
            gate = g_ref[2 * half + head]
            memory = memory_of(mem_ref, 2 * half + head)
            for i in range(4):
                rows = slice(i * SHARE, (i + 1) * SHARE)
                q, y = qs[rows, cs].astype(f32), ys[rows, cs]
                _, _, retrieved, denom_grad, weight = read_rows(memory, gate, q, y)
                out, dq = results_of_rows(
                    memory, gate, q, y, retrieved, denom_grad, weight,
                    local_ref[rows, cs], dq_ref[rows, cs],
                )
                dkv_ref[2, rows, cs] = out
                dkv_ref[3, rows, cs] = dq
        return carry

    lax.fori_loop(0, 2, one_head, 0)
    if half:
        run_copies(
            [
                pltpu.make_async_copy(
                    dkv_ref.at[:, pl.ds(pl.multiple_of(group_of(z, i) * SHARE, SHARE), SHARE)],
                    out,
                    sem_out.at[i],
                )
                for i, out in enumerate(outs)
            ]
        )


def attention(z, gates, arrays, received, half, memory=()):
    seg_half = (SEG, HALF)
    last = [
        pltpu.SemaphoreType.DMA((4,)),
        pltpu.VMEM((4, SEG, HALF), bf16),
        pltpu.VMEM(seg_half, f32),
        pltpu.VMEM(seg_half, f32),
    ]
    return pl.pallas_call(
        functools.partial(attention_kernel, half=half),
        out_shape=[shape((4, SHARE, HALF))] * 4
        if half
        else [shape(seg_half, f32)] * 2 + [shape((2, SEG, HALF))],
        in_specs=[SMEM, SMEM] + [HBM] * 7 + [VMEM] * half,
        out_specs=[HBM] * 4 if half else [VMEM] * 3,
        scratch_shapes=[pltpu.VMEM(seg_half, bf16)] * 4
        + [pltpu.VMEM((DH, SEG), f32)] * 2
        + [pltpu.SemaphoreType.DMA((4, 4))]
        + last * half,
        compiler_params=params(),
        cost_estimate=cost(12 if half else 10),
    )(z, gates, *arrays, *received, *memory)


def memory_kernel(*refs, half, grads, results):
    z_ref, g_ref, mem_ref, q_ref, y_ref, r1, r2, r3 = refs[:8]
    refs = list(refs[8:])
    local_ref, dq_ref, dkv_ref = [refs.pop(0) for _ in range(3)] if results else [None] * 3
    earlier = refs.pop(0) if grads and half else None
    mg_ref = refs.pop(0) if grads else None
    outs = [refs.pop(0) for _ in range(4)] if results else None
    qs, ys, sem = refs[:3]
    ls, ds, kvs, sem_f = refs[3:] if results else [None] * 4
    z = z_ref[0]
    own = pl.ds(pl.multiple_of(z * GROUP + half * HALF, HALF), HALF)
    copies = []
    for shift in range(4):
        for i, (src, dst) in enumerate(((q_ref, qs), (y_ref, ys))):
            block = src.at[:, own] if shift == 0 else (r1, r2, r3)[shift - 1].at[2 + i]
            copies.append(pltpu.make_async_copy(block, dst.at[shift], sem.at[shift, i]))
        if results:
            rows = pl.ds(pl.multiple_of(group_of(z, -shift) * SHARE, SHARE), SHARE)
            for i, (src, dst) in enumerate(
                ((local_ref.at[rows], ls), (dq_ref.at[rows], ds), (dkv_ref.at[:, rows], kvs))
            ):
                copies.append(pltpu.make_async_copy(src, dst.at[shift], sem_f.at[shift, i]))
    run_copies(copies)
    if results:
        outs = [outs[(4 - shift) % 4] for shift in range(4)]
        for shift in range(4):
            outs[shift][:2] = kvs[shift]
    if earlier is not None:
        mg_ref[:16] = earlier[...]
    start = 16 if earlier is not None else 0

    def one_head(head, carry):
        cs = pl.ds(pl.multiple_of(head * DH, DH), DH)
        gate = g_ref[2 * half + head]
        memory = memory_of(mem_ref, 2 * half + head)
        grad = jnp.zeros((DH, 2 * DH), f32)
        norm_grad = jnp.zeros((1, DH), f32)
        for shift in range(4):
            q, y = qs[shift, :, cs].astype(f32), ys[shift, :, cs]
            phi_low, phi, retrieved, denom_grad, weight = read_rows(memory, gate, q, y)
            if grads:
                scaled = split(y.astype(f32) * weight)
                grad += dot(phi_low, jnp.concatenate(scaled, 1), 0, 0)
                norm_grad += jnp.sum(phi * denom_grad, 0, keepdims=True)
            if results:
                out, dq = results_of_rows(
                    memory, gate, q, y, retrieved, denom_grad, weight,
                    ls[shift, :, cs], ds[shift, :, cs],
                )
                outs[shift][2, :, cs] = out
                outs[shift][3, :, cs] = dq
        if grads:
            total = grad[:, :DH] + grad[:, DH:]
            at = pl.multiple_of(start + head * 8, 8)
            mg_ref[pl.ds(at, 8), :16, :] = total.reshape(8, 16, DH).astype(bf16)
            mg_ref[at, 16:32, :] = jnp.broadcast_to(norm_grad, (16, DH)).astype(bf16)
        return carry

    lax.fori_loop(0, 2, one_head, 0)


def read_memory(z, gates, memory, q, y, received, half, earlier=None, local=None, grads=True):
    results = local is not None
    join = grads and half
    out = pl.pallas_call(
        functools.partial(memory_kernel, half=half, grads=grads, results=results),
        out_shape=[shape((32 if half else 16, 32, DH))] * grads
        + [shape((4, SHARE, HALF))] * (4 * results),
        in_specs=[SMEM, SMEM, VMEM] + [HBM] * 5 + [HBM] * (3 * results) + [VMEM] * bool(join),
        out_specs=[VMEM] * (grads + 4 * results),
        scratch_shapes=[pltpu.VMEM((4, SHARE, HALF), bf16)] * 2
        + [pltpu.SemaphoreType.DMA((4, 2))]
        + (
            [pltpu.VMEM((4, SHARE, HALF), f32)] * 2
            + [pltpu.VMEM((4, 2, SHARE, HALF), bf16), pltpu.SemaphoreType.DMA((4, 3))]
        )
        * results,
        compiler_params=params(),
        cost_estimate=cost(4),
    )(z, gates, memory, q, y, *received, *(local or ()), *([earlier] if join else []))
    return (out[0], out[1:]) if grads else out


def token_kernel(z_ref, *rest):
    firsts, seconds, (a_ref, b_ref) = rest[:4], rest[4:8], rest[8:]
    for shift in range(4):
        base = group_of(z_ref[0], -shift) * GROUP
        for half, pieces in enumerate((firsts, seconds)):
            cols = pl.ds(pl.multiple_of(base + half * HALF, HALF), HALF)
            a_ref[:, cols] = pieces[shift][0]
            b_ref[:, cols] = pieces[shift][1]


def results_of_tokens(z, firsts, seconds):
    piece = pl.BlockSpec((2, SHARE, HALF), lambda i: (1, 0, 0))
    whole = pl.BlockSpec((SHARE, 4 * GROUP), lambda i: (0, 0))
    return pl.pallas_call(
        token_kernel,
        grid=(1,),
        out_shape=[shape((SHARE, 4 * GROUP))] * 2,
        in_specs=[SMEM] + [piece] * 8,
        out_specs=[whole] * 2,
        compiler_params=params(),
        cost_estimate=cost(3),
        name="results",
    )(z, *firsts, *seconds)


def compact_kernel(in_ref, out_ref):
    out_ref[:GROUP] = in_ref[:, :16, :].reshape(GROUP, DH)
    for head in range(HEADS):
        out_ref[GROUP + 16 * head : GROUP + 16 * head + 16] = in_ref[8 * head, 16:32, :]


def compact(x):
    return pl.pallas_call(
        compact_kernel,
        out_shape=shape((ROWS, DH)),
        in_specs=[VMEM],
        out_specs=VMEM,
        compiler_params=params(),
        cost_estimate=cost(2),
        name="compact",
    )(x)


def key_value_kernel(z_ref, k_ref, v_ref, *rest):
    backs, firsts, seconds = rest[:4], rest[4:8], rest[8:12]
    kg_ref, vg_ref = rest[12:]
    for shift in range(4):
        base = group_of(z_ref[0], -shift) * GROUP
        for head in range(HEADS):
            cols = pl.ds(pl.multiple_of(base + head * DH, DH), DH)
            inner = slice((head % 2) * DH, (head % 2 + 1) * DH)
            grads = (firsts, seconds)[head // 2][shift]
            back = backs[shift][head * DH : (head + 1) * DH]
            norm = backs[shift][GROUP + 16 * head : GROUP + 16 * head + 16].astype(f32)[:1]
            k = k_ref[:, cols].astype(f32)
            v = v_ref[:, cols]
            kg = grads[0, :, inner].astype(f32) + (dot(v, back, 1, 1) + norm) * slope(k)
            kg_ref[:, cols] = kg.astype(bf16)
            vg = grads[1, :, inner].astype(f32) + dot(feature(k).astype(bf16), back, 1, 0)
            vg_ref[:, cols] = vg.astype(bf16)


def key_value(z, keys, values, backs, firsts, seconds):
    piece = pl.BlockSpec((2, SHARE, HALF), lambda i: (0, 0, 0))
    whole = pl.BlockSpec((SHARE, 4 * GROUP), lambda i: (0, 0))
    state = pl.BlockSpec((ROWS, DH), lambda i: (0, 0))
    return pl.pallas_call(
        key_value_kernel,
        grid=(1,),
        out_shape=[shape((SHARE, 4 * GROUP))] * 2,
        in_specs=[SMEM] + [whole] * 2 + [state] * 4 + [piece] * 8,
        out_specs=[whole] * 2,
        compiler_params=params(),
        cost_estimate=cost(5),
        name="key_value",
    )(z, keys, values, *backs, *firsts, *seconds)


def to_peers(blocks):
    sent = []
    for shift, block in enumerate(blocks, 1):
        sent.append(lax.ppermute(block, "head", [(i, (i + shift) % 4) for i in range(4)]))
    return sent


def swap(x):
    return lax.all_to_all(x, "seq", 0, 0, tiled=True)


def body(k, v, q, y, gate_logits):
    z = lax.axis_index("head").astype(jnp.int32).reshape(1)
    gates = jax.nn.sigmoid(gate_logits)
    arrays = (k, v, q, y)
    partials, own, firsts, seconds = front(z, *arrays)
    partials = to_peers(partials)
    in_a = to_peers(firsts)
    in_b = to_peers(seconds)
    slices = swap(update(own, partials))
    memory = swap(scan(slices, False))
    local_a = attention(z, gates, arrays, in_a, 0)
    grads, out_a = read_memory(z, gates, memory, q, y, in_a, 0, local=local_a)
    back_a = to_peers(out_a[1:])
    grads, _ = read_memory(z, gates, memory, q, y, in_b, 1, earlier=grads)
    slices = swap(grads)
    out_b = attention(z, gates, arrays, in_b, 1, [memory])
    back_b = to_peers(out_b[1:])
    state = compact(swap(scan(slices, True)))
    states = [state] + to_peers([state] * 3)
    firsts, seconds = [out_a[0], *back_a], [out_b[0], *back_b]
    output, query_grad = results_of_tokens(z, firsts, seconds)
    key_grad, value_grad = key_value(z, k, v, states, firsts, seconds)
    return output, query_grad, key_grad, value_grad


def whole(queries, key_rows, values, gate_logits, out_grad):
    return body(key_rows, values, queries, out_grad, gate_logits)


def solution(mesh):
    spec = P(("seq", "head"), None)
    return jax.shard_map(
        whole,
        mesh=mesh,
        in_specs=(spec, spec, spec, P("head"), spec),
        out_specs=(spec,) * 4,
        check_vma=False,
    )
```

profile of v0, /device:TPU:0, one launch (start us, length us, event | category | flops | bytes accessed | tf_op | source)
XLA Modules:
  0.0 159.9 jit_solution(8191089145798534445)
XLA Ops:
  0.6 6.3 %front.1 = (bf16[576,128]{1,0:T(8,128)(2,1)}, bf16[576,128]{1,0:T(8,128)(2,1)}, bf16[576,128]{1,0:T(8,128)(2,1)}, f32[576,128]{1,0:T(8,128)}, bf16[4,256,256]{2,...) custom-call(s32[1]{0:T(128)} %bitcast.z_ref.refs_0_, ...), custom_call_target="tpu_custom_call" | custom-call | flops 3000000000 | bytes 12000000 | tf_op jit(solution)/shard_map/front/pallas_call | solution.py:118
  6.9 2.1 %collective-permute-start = (bf16[576,128]{1,0:T(8,128)(2,1)}, bf16[576,128]{1,0:T(8,128)(2,1)S(1)}, u32[]{:S(2)}, u32[]{:S(2)}) collective-permute-start(bf16[576,128]{1,0:T(8,128)(2,1)} %get-tuple-element.31), channel_id=1, source_target_pairs={{0,1},{1,2},{2,3},{3,0},{4,5},{5,6},{6,7},{7,4},{8,9},{9,10},{10,1... | collective-permute-start | bytes 442376 | tf_op jit(solution)/shard_map/ppermute | solution.py:487
  9.0 3.6 %collective-permute-start.1 = (bf16[576,128]{1,0:T(8,128)(2,1)}, bf16[576,128]{1,0:T(8,128)(2,1)S(1)}, u32[]{:S(2)}, u32[]{:S(2)}) collective-permute-start(bf16[576,128]{1,0:T(8,128)(2,1)} %get-tuple-element.32), channel_id=1, source_target_pairs={{0,2},{1,3},{2,0},{3,1},{4,6},{5,7},{6,4},{7,5},{8,10},{9,11},{10,... | collective-permute-start | bytes 442376 | tf_op jit(solution)/shard_map/ppermute | solution.py:487
  13.6 1.0 collective-permute-start.3
  15.2 2.9 %collective-permute-start.5 = (bf16[4,256,256]{2,1,0:T(8,128)(2,1)}, bf16[4,256,256]{2,1,0:T(8,128)(2,1)S(1)}, u32[]{:S(2)}, u32[]{:S(2)}) collective-permute-start(bf16[4,256,256]{2,1,0:T(8,128)(2,1)} %get-tuple-element.36), channel_id=1, source_target_pairs={{0,3},{1,0},{2,1},{3,2},{4,7},{5,4},{6,5},{7,6},{8,11},{9,8},{10,9... | collective-permute-start | bytes 1572872 | tf_op jit(solution)/shard_map/ppermute | solution.py:487
  18.1 2.6 %collective-permute-done.1.r2 = bf16[576,128]{1,0:T(8,128)(2,1)S(1)} collective-permute-done((bf16[576,128]{1,0:T(8,128)(2,1)}, bf16[576,128]{1,0:T(8,128)(2,1)S(1)}, u32[]{:S(2)}, u32[]{:S(2)}) %collective-permute-start.1) | collective-permute-done | bytes 147488 | tf_op jit(solution)/shard_map/ppermute | solution.py:487
  20.7 8.2 %collective-permute-done.2.r3 = bf16[576,128]{1,0:T(8,128)(2,1)S(1)} collective-permute-done((bf16[576,128]{1,0:T(8,128)(2,1)}, bf16[576,128]{1,0:T(8,128)(2,1)S(1)}, u32[]{:S(2)}, u32[]{:S(2)}) %collective-permute-start.2) | collective-permute-done | bytes 147488 | tf_op jit(solution)/shard_map/ppermute | solution.py:487
  29.5 2.0 %update.1 = f32[32,24,128]{2,1,0:T(8,128)} custom-call(f32[576,128]{1,0:T(8,128)} %get-tuple-element.30.own, bf16[576,128]{1,0:T(8,128)(2,1)} %copy-done.17, bf16[576,128]{1,0:T(8,128)(2,1)} %copy-done.18, bf16[576,128]{1,0:T(8,128)(2,1)} %copy-done.19), custom_call_target="tpu_custom_call" | custom-call | flops 1000000000 | bytes 4000000 | tf_op jit(solution)/shard_map/update/pallas_call | solution.py:152
  31.6 7.4 %all-to-all-start = ((f32[32,24,128]{2,1,0:T(8,128)}), f32[32,24,128]{2,1,0:T(8,128)S(1)}, u32[]{:S(2)}, u32[]{:S(2)}) async-start(f32[32,24,128]{2,1,0:T(8,128)} %update.1), calls=%async_computation | async-start | bytes 786432 | tf_op jit(solution)/shard_map/all_to_all | solution.py:492
  39.1 4.9 %collective-permute-start.11 = (bf16[4,256,256]{2,1,0:T(8,128)(2,1)S(1)}, bf16[4,256,256]{2,1,0:T(8,128)(2,1)}, u32[]{:S(2)}, u32[]{:S(2)}) collective-permute-start(bf16[4,256,256]{2,1,0:T(8,128)(2,1)S(1)} %copy-done.8), channel_id=1, source_target_pairs={{0,3},{1,0},{2,1},{3,2},{4,7},{5,4},{6,5},{7,6},{8,11},{9,8},{10,9... | collective-permute-start | bytes 1572872 | tf_op jit(solution)/shard_map/ppermute | solution.py:487
  44.7 4.3 %all-to-all-done.in_ref = f32[32,24,128]{2,1,0:T(8,128)S(1)} async-done(((f32[32,24,128]{2,1,0:T(8,128)}), f32[32,24,128]{2,1,0:T(8,128)S(1)}, u32[]{:S(2)}, u32[]{:S(2)}) %all-to-all-start) | async-done | bytes 393248 | tf_op jit(solution)/shard_map/all_to_all | solution.py:492
  49.7 1.8 %scan_earlier.1 = f32[32,24,128]{2,1,0:T(8,128)} custom-call(f32[32,24,128]{2,1,0:T(8,128)} %copy-done.1), custom_call_target="tpu_custom_call" | custom-call | flops 1000000000 | bytes 4000000 | tf_op jit(solution)/shard_map/scan_earlier/pallas_call | solution.py:173
  51.5 4.1 %all-to-all-start.1 = ((f32[32,24,128]{2,1,0:T(8,128)}), f32[32,24,128]{2,1,0:T(8,128)S(1)}, u32[]{:S(2)}, u32[]{:S(2)}) async-start(f32[32,24,128]{2,1,0:T(8,128)} %scan_earlier.1), calls=%async_computation.1 | async-start | bytes 786432 | tf_op jit(solution)/shard_map/all_to_all | solution.py:492
  57.2 9.5 %shard_map.84 = (f32[1024,256]{1,0:T(8,128)}, f32[1024,256]{1,0:T(8,128)}, bf16[2,1024,256]{2,1,0:T(8,128)(2,1)}) custom-call(s32[1]{0:T(128)} %bitcast.z_ref.refs_0_, f32[4]{0:T(128)} %add_divide_fusion.g_ref.refs_1_, bf16[256,2048]{1,0:T(8,128)(2,1)} %k_ref.7, bf16[256,2048]{1,0:T(8,128)(2,1)} %v_ref.7, bf16[256,2048]{1,0:T(8,128)(2,1)} %refs_3_.3, ...), custom_call_target="tpu_custom_call" | custom-call | flops 5000000000 | bytes 20000000 | tf_op jit(solution)/shard_map/pallas_call | solution.py:307
  68.5 10.9 %shard_map.86 = (bf16[4,256,256]{2,1,0:T(8,128)(2,1)}, bf16[4,256,256]{2,1,0:T(8,128)(2,1)}, bf16[4,256,256]{2,1,0:T(8,128)(2,1)}, bf16[4,256,256]{2,1,0:T(8,128)(2,1)}) custom-call(s32[1]{0:T(128)} %bitcast.z_ref.refs_0_, f32[4]{0:T(128)} %add_divide_fusion.g_ref.refs_1_, bf16[256,2048]{1,0:T(8,128)(2,1)} %k_ref.7, bf16[256,2048]{1,0:T(8,128)(2,1)} %v_ref.7, ...), custom_call_target="tpu_custom_call" | custom-call | flops 6000000000 | bytes 24000000 | tf_op jit(solution)/shard_map/pallas_call | solution.py:307
  79.3 1.4 collective-permute-start.12
  80.7 6.3 %shard_map.85 = (bf16[16,32,128]{2,1,0:T(8,128)(2,1)}, bf16[4,256,256]{2,1,0:T(8,128)(2,1)}, bf16[4,256,256]{2,1,0:T(8,128)(2,1)}, bf16[4,256,256]{2,1,0:T(8,128)(2,1)}, bf16[4,256,256]{2,1,0:T(8,128)(2,1)}) custom-call(s32[1]{0:T(128)} %bitcast.z_ref.refs_0_, f32[4]{0:T(128)} %add_divide_fusion.g_ref.refs_1_, f32[32,24,128]{2,1,0:T(8,128)} %copy-done, ...), custom_call_target="tpu_custom_call" | custom-call | flops 2000000000 | bytes 8000000 | tf_op jit(solution)/shard_map/pallas_call | solution.py:387
  87.0 4.4 %shard_map.87 = bf16[32,32,128]{2,1,0:T(8,128)(2,1)} custom-call(s32[1]{0:T(128)} %bitcast.z_ref.refs_0_, f32[4]{0:T(128)} %add_divide_fusion.g_ref.refs_1_, f32[32,24,128]{2,1,0:T(8,128)} %copy-done, bf16[256,2048]{1,0:T(8,128)(2,1)} %refs_3_.3, bf16[256,2048]{1,0:T(8,128)(2,1)} %refs_4_.3, bf16[4,256,256]{2,1,0:T(8,128)(2,1)} %collective-permute-done.9.r1.refs_5_, ...), custom_call_target="tpu_custom_call" | custom-call | flops 2000000000 | bytes 8000000 | tf_op jit(solution)/shard_map/pallas_call | solution.py:387
  91.5 7.4 %all-to-all-start.2 = ((bf16[32,32,128]{2,1,0:T(8,128)(2,1)}), bf16[32,32,128]{2,1,0:T(8,128)(2,1)S(1)}, u32[]{:S(2)}, u32[]{:S(2)}) async-start(bf16[32,32,128]{2,1,0:T(8,128)(2,1)} %shard_map.87), calls=%async_computation.2 | async-start | bytes 524288 | tf_op jit(solution)/shard_map/all_to_all | solution.py:492
  98.8 3.4 %collective-permute-start.13 = (bf16[4,256,256]{2,1,0:T(8,128)(2,1)}, bf16[4,256,256]{2,1,0:T(8,128)(2,1)S(1)}, u32[]{:S(2)}, u32[]{:S(2)}) collective-permute-start(bf16[4,256,256]{2,1,0:T(8,128)(2,1)} %get-tuple-element.49), channel_id=1, source_target_pairs={{0,2},{1,3},{2,0},{3,1},{4,6},{5,7},{6,4},{7,5},{8,10},{9,11},{10,... | collective-permute-start | bytes 1572872 | tf_op jit(solution)/shard_map/ppermute | solution.py:487
  102.2 2.0 %collective-permute-start.6 = (bf16[4,256,256]{2,1,0:T(8,128)(2,1)}, bf16[4,256,256]{2,1,0:T(8,128)(2,1)S(1)}, u32[]{:S(2)}, u32[]{:S(2)}) collective-permute-start(bf16[4,256,256]{2,1,0:T(8,128)(2,1)} %get-tuple-element.41), channel_id=1, source_target_pairs={{0,1},{1,2},{2,3},{3,0},{4,5},{5,6},{6,7},{7,4},{8,9},{9,10},{10,1... | collective-permute-start | bytes 1572872 | tf_op jit(solution)/shard_map/ppermute | solution.py:487
  104.5 2.5 %collective-permute-start.8 = (bf16[4,256,256]{2,1,0:T(8,128)(2,1)S(1)}, bf16[4,256,256]{2,1,0:T(8,128)(2,1)}, u32[]{:S(2)}, u32[]{:S(2)}) collective-permute-start(bf16[4,256,256]{2,1,0:T(8,128)(2,1)S(1)} %copy-done.10), channel_id=1, source_target_pairs={{0,3},{1,0},{2,1},{3,2},{4,7},{5,4},{6,5},{7,6},{8,11},{9,8},{10,9... | collective-permute-start | bytes 1572872 | tf_op jit(solution)/shard_map/ppermute | solution.py:487
  108.5 1.7 %scan_later.1 = bf16[32,32,128]{2,1,0:T(8,128)(2,1)} custom-call(bf16[32,32,128]{2,1,0:T(8,128)(2,1)} %copy-done.2), custom_call_target="tpu_custom_call" | custom-call | flops 1000000000 | bytes 4000000 | tf_op jit(solution)/shard_map/scan_later/pallas_call | solution.py:173
  110.2 15.7 %all_to_all.20.in_ref = bf16[32,32,128]{2,1,0:T(8,128)(2,1)} all-to-all(bf16[32,32,128]{2,1,0:T(8,128)(2,1)} %scan_later.1), channel_id=1, replica_groups=mesh['seq'=32,'head'=4] {'seq'}, dimensions={0} | all-to-all | bytes 524288 | tf_op jit(solution)/shard_map/all_to_all | solution.py:492
  125.8 1.6 %compact.1.rest_0_ = bf16[576,128]{1,0:T(8,128)(2,1)} custom-call(bf16[32,32,128]{2,1,0:T(8,128)(2,1)} %all_to_all.20.in_ref), custom_call_target="tpu_custom_call" | custom-call | flops 1000000000 | bytes 4000000 | tf_op jit(solution)/shard_map/compact/pallas_call | solution.py:438
  127.5 2.9 %collective-permute-start.16 = (bf16[576,128]{1,0:T(8,128)(2,1)}, bf16[576,128]{1,0:T(8,128)(2,1)S(1)}, u32[]{:S(2)}, u32[]{:S(2)}) collective-permute-start(bf16[576,128]{1,0:T(8,128)(2,1)} %compact.1.rest_0_), channel_id=1, source_target_pairs={{0,2},{1,3},{2,0},{3,1},{4,6},{5,7},{6,4},{7,5},{8,10},{9,11},{10,... | collective-permute-start | bytes 442376 | tf_op jit(solution)/shard_map/ppermute | solution.py:487
  130.3 1.2 collective-permute-start.17
  131.5 6.6 %collective-permute-done.7.rest_2_.rest_6_ = bf16[4,256,256]{2,1,0:T(8,128)(2,1)} collective-permute-done((bf16[4,256,256]{2,1,0:T(8,128)(2,1)S(1)}, bf16[4,256,256]{2,1,0:T(8,128)(2,1)}, u32[]{:S(2)}, u32[]{:S(2)}) %collective-permute-start.7) | collective-permute-done | bytes 524320 | tf_op jit(solution)/shard_map/ppermute | solution.py:487
  138.1 10.5 %collective-permute-done.8.rest_3_.rest_7_ = bf16[4,256,256]{2,1,0:T(8,128)(2,1)} collective-permute-done((bf16[4,256,256]{2,1,0:T(8,128)(2,1)S(1)}, bf16[4,256,256]{2,1,0:T(8,128)(2,1)}, u32[]{:S(2)}, u32[]{:S(2)}) %collective-permute-start.8) | collective-permute-done | bytes 524320 | tf_op jit(solution)/shard_map/ppermute | solution.py:487
  148.6 3.0 %results.1 = (bf16[256,2048]{1,0:T(8,128)(2,1)}, bf16[256,2048]{1,0:T(8,128)(2,1)}) custom-call(s32[1]{0:T(128)} %bitcast.z_ref.refs_0_, bf16[4,256,256]{2,1,0:T(8,128)(2,1)} %get-tuple-element.40.rest_0_.rest_4_, bf16[4,256,256]{2,1,0:T(8,128)(2,1)} %copy-done.13, bf16[4,256,256]{2,1,0:T(8,128)(2,1)} %collective-permute-done.7.rest_2_.rest_6_, ...), custom_call_target="tpu_custom_call" | custom-call | flops 1500000000 | bytes 6000000 | tf_op jit(solution)/shard_map/results/pallas_call | solution.py:419
  151.6 2.6 %collective-permute-done.17.rest_3_ = bf16[576,128]{1,0:T(8,128)(2,1)S(1)} collective-permute-done((bf16[576,128]{1,0:T(8,128)(2,1)}, bf16[576,128]{1,0:T(8,128)(2,1)S(1)}, u32[]{:S(2)}, u32[]{:S(2)}) %collective-permute-start.17) | collective-permute-done | bytes 147488 | tf_op jit(solution)/shard_map/ppermute | solution.py:487
  154.9 5.1 %key_value.1 = (bf16[256,2048]{1,0:T(8,128)(2,1)}, bf16[256,2048]{1,0:T(8,128)(2,1)}) custom-call(s32[1]{0:T(128)} %bitcast.z_ref.refs_0_, bf16[256,2048]{1,0:T(8,128)(2,1)} %k_ref.7, bf16[256,2048]{1,0:T(8,128)(2,1)} %v_ref.7, bf16[576,128]{1,0:T(8,128)(2,1)} %compact.1.rest_0_, bf16[576,128]{1,0:T(8,128)(2,1)} %copy-done.14, bf16[576,128]{1,0:T(8,128)(2,1)} %copy-done.15, ...), custom_call_target="tpu_custom_call" | custom-call | flops 2500000000 | bytes 10000000 | tf_op jit(solution)/shard_map/key_value/pallas_call | solution.py:472
  (65 shorter events, 9.4 us)
Async XLA Ops:
  6.9 8.3 %collective-permute-start = (bf16[576,128]{1,0:T(8,128)(2,1)}, bf16[576,128]{1,0:T(8,128)(2,1)S(1)}, u32[]{:S(2)}, u32[]{:S(2)}) collective-permute-start(bf16[576,128]{1,0:T(8,128)(2,1)} %get-tuple-element.31), channel_id=1, source_target_pairs={{0,1},{1,2},{2,3},{3,0},{4,5},{5,6},{6,7},{7,4},{8,9},{9,10},{10,1... | collective-permute-start | bytes 442376 | tf_op jit(solution)/shard_map/ppermute | solution.py:487
  9.0 11.6 %collective-permute-start.1 = (bf16[576,128]{1,0:T(8,128)(2,1)}, bf16[576,128]{1,0:T(8,128)(2,1)S(1)}, u32[]{:S(2)}, u32[]{:S(2)}) collective-permute-start(bf16[576,128]{1,0:T(8,128)(2,1)} %get-tuple-element.32), channel_id=1, source_target_pairs={{0,2},{1,3},{2,0},{3,1},{4,6},{5,7},{6,4},{7,5},{8,10},{9,11},{10,... | collective-permute-start | bytes 442376 | tf_op jit(solution)/shard_map/ppermute | solution.py:487
  12.6 16.3 %collective-permute-start.2 = (bf16[576,128]{1,0:T(8,128)(2,1)}, bf16[576,128]{1,0:T(8,128)(2,1)S(1)}, u32[]{:S(2)}, u32[]{:S(2)}) collective-permute-start(bf16[576,128]{1,0:T(8,128)(2,1)} %get-tuple-element.33), channel_id=1, source_target_pairs={{0,3},{1,0},{2,1},{3,2},{4,7},{5,4},{6,5},{7,6},{8,11},{9,8},{10,9... | collective-permute-start | bytes 442376 | tf_op jit(solution)/shard_map/ppermute | solution.py:487
  13.6 31.0 %collective-permute-start.3 = (bf16[4,256,256]{2,1,0:T(8,128)(2,1)}, bf16[4,256,256]{2,1,0:T(8,128)(2,1)S(1)}, u32[]{:S(2)}, u32[]{:S(2)}) collective-permute-start(bf16[4,256,256]{2,1,0:T(8,128)(2,1)} %get-tuple-element.34), channel_id=1, source_target_pairs={{0,1},{1,2},{2,3},{3,0},{4,5},{5,6},{6,7},{7,4},{8,9},{9,10},{10,1... | collective-permute-start | bytes 1572872 | tf_op jit(solution)/shard_map/ppermute | solution.py:487
  14.6 41.0 %collective-permute-start.4 = (bf16[4,256,256]{2,1,0:T(8,128)(2,1)}, bf16[4,256,256]{2,1,0:T(8,128)(2,1)S(1)}, u32[]{:S(2)}, u32[]{:S(2)}) collective-permute-start(bf16[4,256,256]{2,1,0:T(8,128)(2,1)} %get-tuple-element.35), channel_id=1, source_target_pairs={{0,2},{1,3},{2,0},{3,1},{4,6},{5,7},{6,4},{7,5},{8,10},{9,11},{10,... | collective-permute-start | bytes 1572872 | tf_op jit(solution)/shard_map/ppermute | solution.py:487
  15.2 13.7 %copy-start.17 = (bf16[576,128]{1,0:T(8,128)(2,1)}, bf16[576,128]{1,0:T(8,128)(2,1)S(1)}, u32[]{:S(2)}) copy-start(bf16[576,128]{1,0:T(8,128)(2,1)S(1)} %collective-permute-done.r1) | copy-start | bytes 442372
  15.2 40.4 %collective-permute-start.5 = (bf16[4,256,256]{2,1,0:T(8,128)(2,1)}, bf16[4,256,256]{2,1,0:T(8,128)(2,1)S(1)}, u32[]{:S(2)}, u32[]{:S(2)}) collective-permute-start(bf16[4,256,256]{2,1,0:T(8,128)(2,1)} %get-tuple-element.36), channel_id=1, source_target_pairs={{0,3},{1,0},{2,1},{3,2},{4,7},{5,4},{6,5},{7,6},{8,11},{9,8},{10,9... | collective-permute-start | bytes 1572872 | tf_op jit(solution)/shard_map/ppermute | solution.py:487
  20.7 8.2 %copy-start.18 = (bf16[576,128]{1,0:T(8,128)(2,1)}, bf16[576,128]{1,0:T(8,128)(2,1)S(1)}, u32[]{:S(2)}) copy-start(bf16[576,128]{1,0:T(8,128)(2,1)S(1)} %collective-permute-done.1.r2) | copy-start | bytes 442372
  29.5 9.6 %copy-start.8 = (bf16[4,256,256]{2,1,0:T(8,128)(2,1)S(1)}, bf16[4,256,256]{2,1,0:T(8,128)(2,1)}, u32[]{:S(2)}) copy-start(bf16[4,256,256]{2,1,0:T(8,128)(2,1)} %get-tuple-element.46) | copy-start | bytes 1572868
  31.6 13.0 %copy-start.6 = (bf16[4,256,256]{2,1,0:T(8,128)(2,1)S(1)}, bf16[4,256,256]{2,1,0:T(8,128)(2,1)}, u32[]{:S(2)}) copy-start(bf16[4,256,256]{2,1,0:T(8,128)(2,1)} %get-tuple-element.44) | copy-start | bytes 1572868
  31.6 17.4 %all-to-all-start = ((f32[32,24,128]{2,1,0:T(8,128)}), f32[32,24,128]{2,1,0:T(8,128)S(1)}, u32[]{:S(2)}, u32[]{:S(2)}) async-start(f32[32,24,128]{2,1,0:T(8,128)} %update.1), calls=%async_computation | async-start | bytes 786432 | tf_op jit(solution)/shard_map/all_to_all | solution.py:492
  39.0 27.7 %collective-permute-start.10 = (bf16[4,256,256]{2,1,0:T(8,128)(2,1)}, bf16[4,256,256]{2,1,0:T(8,128)(2,1)}, u32[]{:S(2)}, u32[]{:S(2)}) collective-permute-start(bf16[4,256,256]{2,1,0:T(8,128)(2,1)} %get-tuple-element.45), channel_id=1, source_target_pairs={{0,2},{1,3},{2,0},{3,1},{4,6},{5,7},{6,4},{7,5},{8,10},{9,11},{10,... | collective-permute-start | bytes 1572872 | tf_op jit(solution)/shard_map/ppermute | solution.py:487
  39.1 28.6 %collective-permute-start.11 = (bf16[4,256,256]{2,1,0:T(8,128)(2,1)S(1)}, bf16[4,256,256]{2,1,0:T(8,128)(2,1)}, u32[]{:S(2)}, u32[]{:S(2)}) collective-permute-start(bf16[4,256,256]{2,1,0:T(8,128)(2,1)S(1)} %copy-done.8), channel_id=1, source_target_pairs={{0,3},{1,0},{2,1},{3,2},{4,7},{5,4},{6,5},{7,6},{8,11},{9,8},{10,9... | collective-permute-start | bytes 1572872 | tf_op jit(solution)/shard_map/ppermute | solution.py:487
  44.6 7.0 %copy-start.4 = (bf16[4,256,256]{2,1,0:T(8,128)(2,1)}, bf16[4,256,256]{2,1,0:T(8,128)(2,1)S(1)}, u32[]{:S(2)}) copy-start(bf16[4,256,256]{2,1,0:T(8,128)(2,1)S(1)} %collective-permute-done.3.r1.refs_5_) | copy-start | bytes 1572868
  44.6 23.2 %collective-permute-start.9 = (bf16[4,256,256]{2,1,0:T(8,128)(2,1)S(1)}, bf16[4,256,256]{2,1,0:T(8,128)(2,1)}, u32[]{:S(2)}, u32[]{:S(2)}) collective-permute-start(bf16[4,256,256]{2,1,0:T(8,128)(2,1)S(1)} %copy-done.6), channel_id=1, source_target_pairs={{0,1},{1,2},{2,3},{3,0},{4,5},{5,6},{6,7},{7,4},{8,9},{9,10},{10,1... | collective-permute-start | bytes 1572872 | tf_op jit(solution)/shard_map/ppermute | solution.py:487
  51.5 16.2 %all-to-all-start.1 = ((f32[32,24,128]{2,1,0:T(8,128)}), f32[32,24,128]{2,1,0:T(8,128)S(1)}, u32[]{:S(2)}, u32[]{:S(2)}) async-start(f32[32,24,128]{2,1,0:T(8,128)} %scan_earlier.1), calls=%async_computation.1 | async-start | bytes 786432 | tf_op jit(solution)/shard_map/all_to_all | solution.py:492
  79.3 25.1 %collective-permute-start.12 = (bf16[4,256,256]{2,1,0:T(8,128)(2,1)}, bf16[4,256,256]{2,1,0:T(8,128)(2,1)S(1)}, u32[]{:S(2)}, u32[]{:S(2)}) collective-permute-start(bf16[4,256,256]{2,1,0:T(8,128)(2,1)} %get-tuple-element.48), channel_id=1, source_target_pairs={{0,1},{1,2},{2,3},{3,0},{4,5},{5,6},{6,7},{7,4},{8,9},{9,10},{10,1... | collective-permute-start | bytes 1572872 | tf_op jit(solution)/shard_map/ppermute | solution.py:487
  87.0 17.2 %copy-start.12 = (bf16[4,256,256]{2,1,0:T(8,128)(2,1)S(1)}, bf16[4,256,256]{2,1,0:T(8,128)(2,1)}, u32[]{:S(2)}) copy-start(bf16[4,256,256]{2,1,0:T(8,128)(2,1)} %get-tuple-element.42) | copy-start | bytes 1572868
  91.5 13.0 %copy-start.10 = (bf16[4,256,256]{2,1,0:T(8,128)(2,1)S(1)}, bf16[4,256,256]{2,1,0:T(8,128)(2,1)}, u32[]{:S(2)}) copy-start(bf16[4,256,256]{2,1,0:T(8,128)(2,1)} %get-tuple-element.43) | copy-start | bytes 1572868
  91.5 16.3 %all-to-all-start.2 = ((bf16[32,32,128]{2,1,0:T(8,128)(2,1)}), bf16[32,32,128]{2,1,0:T(8,128)(2,1)S(1)}, u32[]{:S(2)}, u32[]{:S(2)}) async-start(bf16[32,32,128]{2,1,0:T(8,128)(2,1)} %shard_map.87), calls=%async_computation.2 | async-start | bytes 524288 | tf_op jit(solution)/shard_map/all_to_all | solution.py:492
  98.8 28.6 %collective-permute-start.13 = (bf16[4,256,256]{2,1,0:T(8,128)(2,1)}, bf16[4,256,256]{2,1,0:T(8,128)(2,1)S(1)}, u32[]{:S(2)}, u32[]{:S(2)}) collective-permute-start(bf16[4,256,256]{2,1,0:T(8,128)(2,1)} %get-tuple-element.49), channel_id=1, source_target_pairs={{0,2},{1,3},{2,0},{3,1},{4,6},{5,7},{6,4},{7,5},{8,10},{9,11},{10,... | collective-permute-start | bytes 1572872 | tf_op jit(solution)/shard_map/ppermute | solution.py:487
  102.2 25.2 %collective-permute-start.14 = (bf16[4,256,256]{2,1,0:T(8,128)(2,1)}, bf16[4,256,256]{2,1,0:T(8,128)(2,1)S(1)}, u32[]{:S(2)}, u32[]{:S(2)}) collective-permute-start(bf16[4,256,256]{2,1,0:T(8,128)(2,1)} %get-tuple-element.50), channel_id=1, source_target_pairs={{0,3},{1,0},{2,1},{3,2},{4,7},{5,4},{6,5},{7,6},{8,11},{9,8},{10,9... | collective-permute-start | bytes 1572872 | tf_op jit(solution)/shard_map/ppermute | solution.py:487
  102.2 28.1 %collective-permute-start.6 = (bf16[4,256,256]{2,1,0:T(8,128)(2,1)}, bf16[4,256,256]{2,1,0:T(8,128)(2,1)S(1)}, u32[]{:S(2)}, u32[]{:S(2)}) collective-permute-start(bf16[4,256,256]{2,1,0:T(8,128)(2,1)} %get-tuple-element.41), channel_id=1, source_target_pairs={{0,1},{1,2},{2,3},{3,0},{4,5},{5,6},{6,7},{7,4},{8,9},{9,10},{10,1... | collective-permute-start | bytes 1572872 | tf_op jit(solution)/shard_map/ppermute | solution.py:487
  104.3 33.8 %collective-permute-start.7 = (bf16[4,256,256]{2,1,0:T(8,128)(2,1)S(1)}, bf16[4,256,256]{2,1,0:T(8,128)(2,1)}, u32[]{:S(2)}, u32[]{:S(2)}) collective-permute-start(bf16[4,256,256]{2,1,0:T(8,128)(2,1)S(1)} %copy-done.12), channel_id=1, source_target_pairs={{0,2},{1,3},{2,0},{3,1},{4,6},{5,7},{6,4},{7,5},{8,10},{9,11},{10,... | collective-permute-start | bytes 1572872 | tf_op jit(solution)/shard_map/ppermute | solution.py:487
  104.5 5.7 %copy-start.3 = (bf16[4,256,256]{2,1,0:T(8,128)(2,1)}, bf16[4,256,256]{2,1,0:T(8,128)(2,1)S(1)}, u32[]{:S(2)}) copy-start(bf16[4,256,256]{2,1,0:T(8,128)(2,1)S(1)} %collective-permute-done.12.rest_5_.rest_9_) | copy-start | bytes 1572868
  104.5 44.1 %collective-permute-start.8 = (bf16[4,256,256]{2,1,0:T(8,128)(2,1)S(1)}, bf16[4,256,256]{2,1,0:T(8,128)(2,1)}, u32[]{:S(2)}, u32[]{:S(2)}) collective-permute-start(bf16[4,256,256]{2,1,0:T(8,128)(2,1)S(1)} %copy-done.10), channel_id=1, source_target_pairs={{0,3},{1,0},{2,1},{3,2},{4,7},{5,4},{6,5},{7,6},{8,11},{9,8},{10,9... | collective-permute-start | bytes 1572872 | tf_op jit(solution)/shard_map/ppermute | solution.py:487
  127.4 21.2 %copy-start.9 = (bf16[4,256,256]{2,1,0:T(8,128)(2,1)}, bf16[4,256,256]{2,1,0:T(8,128)(2,1)S(1)}, u32[]{:S(2)}) copy-start(bf16[4,256,256]{2,1,0:T(8,128)(2,1)S(1)} %collective-permute-done.13.rest_6_.rest_10_) | copy-start | bytes 1572868
  127.4 24.2 %collective-permute-start.15 = (bf16[576,128]{1,0:T(8,128)(2,1)}, bf16[576,128]{1,0:T(8,128)(2,1)S(1)}, u32[]{:S(2)}, u32[]{:S(2)}) collective-permute-start(bf16[576,128]{1,0:T(8,128)(2,1)} %compact.1.rest_0_), channel_id=1, source_target_pairs={{0,1},{1,2},{2,3},{3,0},{4,5},{5,6},{6,7},{7,4},{8,9},{9,10},{10,1... | collective-permute-start | bytes 442376 | tf_op jit(solution)/shard_map/ppermute | solution.py:487
  127.5 21.2 %copy-start.11 = (bf16[4,256,256]{2,1,0:T(8,128)(2,1)}, bf16[4,256,256]{2,1,0:T(8,128)(2,1)S(1)}, u32[]{:S(2)}) copy-start(bf16[4,256,256]{2,1,0:T(8,128)(2,1)S(1)} %collective-permute-done.14.rest_7_.rest_11_) | copy-start | bytes 1572868
  127.5 24.1 %collective-permute-start.16 = (bf16[576,128]{1,0:T(8,128)(2,1)}, bf16[576,128]{1,0:T(8,128)(2,1)S(1)}, u32[]{:S(2)}, u32[]{:S(2)}) collective-permute-start(bf16[576,128]{1,0:T(8,128)(2,1)} %compact.1.rest_0_), channel_id=1, source_target_pairs={{0,2},{1,3},{2,0},{3,1},{4,6},{5,7},{6,4},{7,5},{8,10},{9,11},{10,... | collective-permute-start | bytes 442376 | tf_op jit(solution)/shard_map/ppermute | solution.py:487
  130.3 18.3 %copy-start.13 = (bf16[4,256,256]{2,1,0:T(8,128)(2,1)}, bf16[4,256,256]{2,1,0:T(8,128)(2,1)S(1)}, u32[]{:S(2)}) copy-start(bf16[4,256,256]{2,1,0:T(8,128)(2,1)S(1)} %collective-permute-done.6.rest_1_.rest_5_) | copy-start | bytes 1572868
  130.3 23.9 %collective-permute-start.17 = (bf16[576,128]{1,0:T(8,128)(2,1)}, bf16[576,128]{1,0:T(8,128)(2,1)S(1)}, u32[]{:S(2)}, u32[]{:S(2)}) collective-permute-start(bf16[576,128]{1,0:T(8,128)(2,1)} %compact.1.rest_0_), channel_id=1, source_target_pairs={{0,3},{1,0},{2,1},{3,2},{4,7},{5,4},{6,5},{7,6},{8,11},{9,8},{10,9... | collective-permute-start | bytes 442376 | tf_op jit(solution)/shard_map/ppermute | solution.py:487
  (10 other events, 15.3 us)
where the time goes:
time: 161 us; the launch traced here: 160 us
  Pallas kernels  52.5 us (33%)
  starting transfers between devices  48.5 us (30%)
  waiting for transfers between devices  36.6 us (23%)
  blocking collectives  15.7 us (10%)
  local copies, waits for them, and re-layouts  5.15 us (3%)
    ppermute x18, waiting for transfers between devices, to_peers(): lax.ppermute(block, 'head', [(i, (i + shift) % 4) for i in range(4)])  31.6 us
    ppermute x18, starting transfers between devices, to_peers(): lax.ppermute(block, 'head', [(i, (i + shift) % 4) for i in range(4)])  29.7 us
    pallas_call x2, Pallas kernels, attention(): pl.pallas_call(functools.partial(attention_kernel, half=half), out_shape=...  20.4 us
    all_to_all x3, starting transfers between devices, swap(): return lax.all_to_all(x, 'seq', 0, 0, tiled=True)  18.9 us
    all_to_all x1, blocking collectives, swap(): return lax.all_to_all(x, 'seq', 0, 0, tiled=True)  15.7 us
    pallas_call x2, Pallas kernels, read_memory(): pl.pallas_call(functools.partial(memory_kernel, half=half, grads=grads, r...  10.7 us
    pallas_call x1, Pallas kernels, front(): pl.pallas_call(front_kernel, out_shape=[shape((ROWS, DH))] * 3 + [shape((...  6.27 us
    unnamed x42, local copies, waits for them, and re-layouts  5.15 us
  transfers between devices with their start and end apart: 21, of which 9 were waited for; matrix products, arithmetic and copies ran while one was open for 0% of the time, Pallas kernels for 19%

commit v1 on v0

--- a/solution.py
+++ b/solution.py
@@ -66,34 +66,32 @@
 
 
 def front_kernel(z_ref, k_ref, v_ref, q_ref, y_ref, *rest):
-    partials, own_ref, firsts, seconds = rest[:3], rest[3], rest[4:7], rest[7:10]
-    buf, sem_in, sem_out = rest[10:]
+    partials, own_ref, outs = rest[:3], rest[3], (rest[4:7], rest[7:10], rest[10:13])
+    buf, sem_in, sem_out = rest[13:]
     z = z_ref[0]
-    loads, stores = [], []
+    loads, late, stores = [], [], []
     for shift in (1, 2, 3):
         at = pl.multiple_of(group_of(z, shift) * GROUP, GROUP)
-        for i, src in enumerate((k_ref, v_ref, q_ref, y_ref)):
-            here = (shift - 1, i)
-            for half, outs in enumerate((firsts, seconds)):
-                cols = pl.ds(half * HALF, HALF)
-                stores.append(
-                    pltpu.make_async_copy(
-                        buf.at[shift - 1, i, :, cols],
-                        outs[shift - 1].at[i],
-                        sem_out.at[shift - 1, i, half],
-                    )
+        first, queries, keys = [group[shift - 1] for group in outs]
+        for i, src in enumerate((k_ref, v_ref)):
+            sem = sem_out.at[shift - 1, i]
+            cols = pl.ds(at, HALF)
+            stores.append(pltpu.make_async_copy(src.at[:, cols], first.at[i], sem.at[0]))
+            cols = pl.ds(pl.multiple_of(at + HALF, HALF), HALF)
+            stores.append(pltpu.make_async_copy(src.at[:, cols], keys.at[i], sem.at[1]))
+        for i, src in enumerate((q_ref, y_ref)):
+            part, sem = buf.at[shift - 1, i], sem_out.at[shift - 1, 2 + i]
+            cols = pl.ds(at, GROUP)
+            loads.append(pltpu.make_async_copy(src.at[:, cols], part, sem_in.at[shift - 1, i]))
+            late.append(
+                (
+                    pltpu.make_async_copy(part.at[:, pl.ds(0, HALF)], first.at[2 + i], sem.at[0]),
+                    pltpu.make_async_copy(part.at[:, pl.ds(HALF, HALF)], queries.at[i], sem.at[1]),
                 )
-            if i >= 2:
-                copy = pltpu.make_async_copy(
-                    src.at[:, pl.ds(at, GROUP)], buf.at[here], sem_in.at[shift - 1, i - 2]
-                )
-                copy.start()
-                loads.append(copy)
-            else:
-                buf[here] = src[:, pl.ds(at, GROUP)]
-                stores[-1].start()
-                stores[-2].start()
-    for shift in (1, 2, 3, 0):
+            )
+    for copy in loads + stores:
+        copy.start()
+    for step, shift in enumerate((1, 2, 3, 0)):
         base = group_of(z, shift) * GROUP
         out = own_ref if shift == 0 else partials[shift - 1]
         for head in range(HEADS):
@@ -105,11 +103,12 @@
             first = lax.broadcasted_iota(jnp.int32, (16, DH), 0) == 0
             rows = jnp.where(first, jnp.broadcast_to(high, (16, DH)), sums - high)
             out[GROUP + 16 * head : GROUP + 16 * head + 16] = rows.astype(out.dtype)
-    for j, copy in enumerate(loads):
-        copy.wait()
-        at = 8 * (j // 2) + 2 * (2 + j % 2)
-        stores[at].start()
-        stores[at + 1].start()
+        if step == 1:
+            for copy, pair in zip(loads, late):
+                copy.wait()
+                for store in pair:
+                    store.start()
+                    stores.append(store)
     for copy in stores:
         copy.wait()
 
@@ -119,19 +118,20 @@
         front_kernel,
         out_shape=[shape((ROWS, DH))] * 3
         + [shape((ROWS, DH), f32)]
-        + [shape((4, SHARE, HALF))] * 6,
+        + [shape((4, SHARE, HALF))] * 3
+        + [shape((2, SHARE, HALF))] * 6,
         in_specs=[SMEM, VMEM, VMEM, HBM, HBM],
-        out_specs=[VMEM] * 4 + [HBM] * 6,
+        out_specs=[VMEM] * 4 + [HBM] * 9,
         scratch_shapes=[
-            pltpu.VMEM((3, 4, SHARE, GROUP), bf16),
+            pltpu.VMEM((3, 2, SHARE, GROUP), bf16),
             pltpu.SemaphoreType.DMA((3, 2)),
             pltpu.SemaphoreType.DMA((3, 4, 2)),
         ],
-        compiler_params=params(),
+        compiler_params=params(60),
         cost_estimate=cost(6),
         name="front",
     )(z, k, v, q, y)
-    return out[:3], out[3], out[4:7], out[7:10]
+    return out[:3], out[3], out[4:7], out[7:10], out[10:13]
 
 
 def update_kernel(own, r1, r2, r3, out_ref):
@@ -154,28 +154,43 @@
         out_shape=shape((32, 24, DH), f32),
         in_specs=[VMEM] * 4,
         out_specs=VMEM,
-        compiler_params=params(),
+        compiler_params=params(8),
         cost_estimate=cost(2),
         name="update",
     )(own, *received)
 
 
-def scan_kernel(in_ref, out_ref, *, reverse):
-    count = in_ref.shape[0]
+def scan_kernel(in_ref, out_ref, buf, res, sem_in, sem_out, *, reverse):
+    count, parts = in_ref.shape[0], 4
+    each = count // parts
+    order = list(range(parts))[::-1] if reverse else list(range(parts))
+    loads, stores = [], []
+    for part in range(parts):
+        at = pl.ds(part * each, each)
+        loads.append(pltpu.make_async_copy(in_ref.at[at], buf.at[at], sem_in.at[part]))
+        stores.append(pltpu.make_async_copy(res.at[at], out_ref.at[at], sem_out.at[part]))
+    for part in order:
+        loads[part].start()
     total = jnp.zeros(in_ref.shape[1:], f32)
-    for step in range(count):
-        at = count - 1 - step if reverse else step
-        out_ref[at] = total.astype(out_ref.dtype)
-        total += in_ref[at].astype(f32)
+    for part in order:
+        loads[part].wait()
+        for step in range(each):
+            at = part * each + (each - 1 - step if reverse else step)
+            res[at] = total.astype(res.dtype)
+            total += buf[at].astype(f32)
+        stores[part].start()
+    for copy in stores:
+        copy.wait()
 
 
 def scan(x, reverse):
     return pl.pallas_call(
         functools.partial(scan_kernel, reverse=reverse),
         out_shape=shape(x.shape, x.dtype),
-        in_specs=[VMEM],
-        out_specs=VMEM,
-        compiler_params=params(),
+        in_specs=[HBM],
+        out_specs=HBM,
+        scratch_shapes=[pltpu.VMEM(x.shape, x.dtype)] * 2 + [pltpu.SemaphoreType.DMA((4,))] * 2,
+        compiler_params=params(12),
         cost_estimate=cost(2),
         name="scan_later" if reverse else "scan_earlier",
     )(x)
@@ -213,9 +228,10 @@
 
 
 def attention_kernel(
-    z_ref, g_ref, k_ref, v_ref, q_ref, y_ref, r1, r2, r3, *refs, half
+    z_ref, g_ref, k_ref, v_ref, q_ref, y_ref, *refs, half
 ):
     refs = list(refs)
+    received = [[refs.pop(0) for _ in range(3)] for _ in range(1 + half)]
     mem_ref = refs.pop(0) if half else None
     if half:
         outs = [refs.pop(0) for _ in range(4)]
@@ -229,7 +245,12 @@
     for shift in range(4):
         rows = pl.ds(pl.multiple_of(group_of(z, -shift) * SHARE, SHARE), SHARE)
         for i, (src, dst) in enumerate(zip((k_ref, v_ref, q_ref, y_ref), (ks, vs, qs, ys))):
-            block = src.at[:, own] if shift == 0 else (r1, r2, r3)[shift - 1].at[i]
+            if shift == 0:
+                block = src.at[:, own]
+            elif half:
+                block = received[i // 2][shift - 1].at[i % 2]
+            else:
+                block = received[0][shift - 1].at[i]
             copies.append(pltpu.make_async_copy(block, dst.at[rows], sem.at[shift, i]))
     run_copies(copies)
 
@@ -309,61 +330,61 @@
         out_shape=[shape((4, SHARE, HALF))] * 4
         if half
         else [shape(seg_half, f32)] * 2 + [shape((2, SEG, HALF))],
-        in_specs=[SMEM, SMEM] + [HBM] * 7 + [VMEM] * half,
+        in_specs=[SMEM, SMEM] + [HBM] * (4 + 3 * (1 + half)) + [VMEM] * half,
         out_specs=[HBM] * 4 if half else [VMEM] * 3,
         scratch_shapes=[pltpu.VMEM(seg_half, bf16)] * 4
         + [pltpu.VMEM((DH, SEG), f32)] * 2
         + [pltpu.SemaphoreType.DMA((4, 4))]
         + last * half,
-        compiler_params=params(),
+        compiler_params=params(60),
         cost_estimate=cost(12 if half else 10),
     )(z, gates, *arrays, *received, *memory)
 
 
-def memory_kernel(*refs, half, grads, results):
-    z_ref, g_ref, mem_ref, q_ref, y_ref, r1, r2, r3 = refs[:8]
-    refs = list(refs[8:])
-    local_ref, dq_ref, dkv_ref = [refs.pop(0) for _ in range(3)] if results else [None] * 3
-    earlier = refs.pop(0) if grads and half else None
-    mg_ref = refs.pop(0) if grads else None
-    outs = [refs.pop(0) for _ in range(4)] if results else None
-    qs, ys, sem = refs[:3]
-    ls, ds, kvs, sem_f = refs[3:] if results else [None] * 4
+def memory_kernel(
+    z_ref, g_ref, mem_ref, q_ref, y_ref, a1, a2, a3, b1, b2, b3, local_ref, dq_ref, dkv_ref,
+    mg_ref, o0, o1, o2, o3,
+    qs, ys, ls, ds, kvs, sem, sem_f
+):
     z = z_ref[0]
-    own = pl.ds(pl.multiple_of(z * GROUP + half * HALF, HALF), HALF)
+    own = pl.ds(pl.multiple_of(z * GROUP, GROUP), GROUP)
     copies = []
     for shift in range(4):
         for i, (src, dst) in enumerate(((q_ref, qs), (y_ref, ys))):
-            block = src.at[:, own] if shift == 0 else (r1, r2, r3)[shift - 1].at[2 + i]
-            copies.append(pltpu.make_async_copy(block, dst.at[shift], sem.at[shift, i]))
-        if results:
-            rows = pl.ds(pl.multiple_of(group_of(z, -shift) * SHARE, SHARE), SHARE)
-            for i, (src, dst) in enumerate(
-                ((local_ref.at[rows], ls), (dq_ref.at[rows], ds), (dkv_ref.at[:, rows], kvs))
+            if shift == 0:
+                copies.append(
+                    pltpu.make_async_copy(src.at[:, own], dst.at[0], sem.at[0, i, 0])
+                )
+                continue
+            for half, block in enumerate(
+                ((a1, a2, a3)[shift - 1].at[2 + i], (b1, b2, b3)[shift - 1].at[i])
             ):
-                copies.append(pltpu.make_async_copy(src, dst.at[shift], sem_f.at[shift, i]))
+                cols = pl.ds(half * HALF, HALF)
+                copies.append(
+                    pltpu.make_async_copy(block, dst.at[shift, :, cols], sem.at[shift, i, half])
+                )
+        rows = pl.ds(pl.multiple_of(group_of(z, -shift) * SHARE, SHARE), SHARE)
+        for i, (src, dst) in enumerate(
+            ((local_ref.at[rows], ls), (dq_ref.at[rows], ds), (dkv_ref.at[:, rows], kvs))
+        ):
+            copies.append(pltpu.make_async_copy(src, dst.at[shift], sem_f.at[shift, i]))
     run_copies(copies)
-    if results:
-        outs = [outs[(4 - shift) % 4] for shift in range(4)]
-        for shift in range(4):
-            outs[shift][:2] = kvs[shift]
-    if earlier is not None:
-        mg_ref[:16] = earlier[...]
-    start = 16 if earlier is not None else 0
-
-    def one_head(head, carry):
+    outs = (o0, o3, o2, o1)
+    for shift in range(4):
+        outs[shift][:2] = kvs[shift]
+
+    def one_head(head, carry, results):
         cs = pl.ds(pl.multiple_of(head * DH, DH), DH)
-        gate = g_ref[2 * half + head]
-        memory = memory_of(mem_ref, 2 * half + head)
+        gate = g_ref[head]
+        memory = memory_of(mem_ref, head)
         grad = jnp.zeros((DH, 2 * DH), f32)
         norm_grad = jnp.zeros((1, DH), f32)
         for shift in range(4):
             q, y = qs[shift, :, cs].astype(f32), ys[shift, :, cs]
             phi_low, phi, retrieved, denom_grad, weight = read_rows(memory, gate, q, y)
-            if grads:
-                scaled = split(y.astype(f32) * weight)
-                grad += dot(phi_low, jnp.concatenate(scaled, 1), 0, 0)
-                norm_grad += jnp.sum(phi * denom_grad, 0, keepdims=True)
+            scaled = split(y.astype(f32) * weight)
+            grad += dot(phi_low, jnp.concatenate(scaled, 1), 0, 0)
+            norm_grad += jnp.sum(phi * denom_grad, 0, keepdims=True)
             if results:
                 out, dq = results_of_rows(
                     memory, gate, q, y, retrieved, denom_grad, weight,
@@ -371,36 +392,34 @@
                 )
                 outs[shift][2, :, cs] = out
                 outs[shift][3, :, cs] = dq
-        if grads:
-            total = grad[:, :DH] + grad[:, DH:]
-            at = pl.multiple_of(start + head * 8, 8)
-            mg_ref[pl.ds(at, 8), :16, :] = total.reshape(8, 16, DH).astype(bf16)
-            mg_ref[at, 16:32, :] = jnp.broadcast_to(norm_grad, (16, DH)).astype(bf16)
+        total = grad[:, :DH] + grad[:, DH:]
+        at = pl.multiple_of(head * 8, 8)
+        mg_ref[pl.ds(at, 8), :16, :] = total.reshape(8, 16, DH).astype(bf16)
+        mg_ref[at, 16:32, :] = jnp.broadcast_to(norm_grad, (16, DH)).astype(bf16)
         return carry
 
-    lax.fori_loop(0, 2, one_head, 0)
-
-
-def read_memory(z, gates, memory, q, y, received, half, earlier=None, local=None, grads=True):
-    results = local is not None
-    join = grads and half
+    lax.fori_loop(0, 2, functools.partial(one_head, results=True), 0)
+    lax.fori_loop(2, 4, functools.partial(one_head, results=False), 0)
+
+
+def read_memory(z, gates, memory, q, y, in_a, qy_b, local):
     out = pl.pallas_call(
-        functools.partial(memory_kernel, half=half, grads=grads, results=results),
-        out_shape=[shape((32 if half else 16, 32, DH))] * grads
-        + [shape((4, SHARE, HALF))] * (4 * results),
-        in_specs=[SMEM, SMEM, VMEM] + [HBM] * 5 + [HBM] * (3 * results) + [VMEM] * bool(join),
-        out_specs=[VMEM] * (grads + 4 * results),
-        scratch_shapes=[pltpu.VMEM((4, SHARE, HALF), bf16)] * 2
-        + [pltpu.SemaphoreType.DMA((4, 2))]
-        + (
-            [pltpu.VMEM((4, SHARE, HALF), f32)] * 2
-            + [pltpu.VMEM((4, 2, SHARE, HALF), bf16), pltpu.SemaphoreType.DMA((4, 3))]
-        )
-        * results,
-        compiler_params=params(),
-        cost_estimate=cost(4),
-    )(z, gates, memory, q, y, *received, *(local or ()), *([earlier] if join else []))
-    return (out[0], out[1:]) if grads else out
+        memory_kernel,
+        out_shape=[shape((32, 32, DH))] + [shape((4, SHARE, HALF))] * 4,
+        in_specs=[SMEM, SMEM, VMEM] + [HBM] * 11,
+        out_specs=[VMEM] * 5,
+        scratch_shapes=[pltpu.VMEM((4, SHARE, GROUP), bf16)] * 2
+        + [pltpu.VMEM((4, SHARE, HALF), f32)] * 2
+        + [
+            pltpu.VMEM((4, 2, SHARE, HALF), bf16),
+            pltpu.SemaphoreType.DMA((4, 2, 2)),
+            pltpu.SemaphoreType.DMA((4, 3)),
+        ],
+        compiler_params=params(60),
+        cost_estimate=cost(8),
+        name="read_memory",
+    )(z, gates, memory, q, y, *in_a, *qy_b, *local)
+    return out[0], out[1:]
 
 
 def token_kernel(z_ref, *rest):
@@ -422,7 +441,7 @@
         out_shape=[shape((SHARE, 4 * GROUP))] * 2,
         in_specs=[SMEM] + [piece] * 8,
         out_specs=[whole] * 2,
-        compiler_params=params(),
+        compiler_params=params(16),
         cost_estimate=cost(3),
         name="results",
     )(z, *firsts, *seconds)
@@ -440,7 +459,7 @@
         out_shape=shape((ROWS, DH)),
         in_specs=[VMEM],
         out_specs=VMEM,
-        compiler_params=params(),
+        compiler_params=params(8),
         cost_estimate=cost(2),
         name="compact",
     )(x)
@@ -450,32 +469,37 @@
     backs, firsts, seconds = rest[:4], rest[4:8], rest[8:12]
     kg_ref, vg_ref = rest[12:]
     for shift in range(4):
-        base = group_of(z_ref[0], -shift) * GROUP
-        for head in range(HEADS):
-            cols = pl.ds(pl.multiple_of(base + head * DH, DH), DH)
-            inner = slice((head % 2) * DH, (head % 2 + 1) * DH)
-            grads = (firsts, seconds)[head // 2][shift]
-            back = backs[shift][head * DH : (head + 1) * DH]
-            norm = backs[shift][GROUP + 16 * head : GROUP + 16 * head + 16].astype(f32)[:1]
-            k = k_ref[:, cols].astype(f32)
-            v = v_ref[:, cols]
-            kg = grads[0, :, inner].astype(f32) + (dot(v, back, 1, 1) + norm) * slope(k)
-            kg_ref[:, cols] = kg.astype(bf16)
-            vg = grads[1, :, inner].astype(f32) + dot(feature(k).astype(bf16), back, 1, 0)
-            vg_ref[:, cols] = vg.astype(bf16)
+
+        @pl.when(pl.program_id(0) == shift)
+        def _():
+            for head in range(HEADS):
+                cols = slice(head * DH, (head + 1) * DH)
+                inner = slice((head % 2) * DH, (head % 2 + 1) * DH)
+                grads = (firsts, seconds)[head // 2][shift]
+                back = backs[shift][cols]
+                norm = backs[shift][GROUP + 16 * head : GROUP + 16 * head + 16].astype(f32)[:1]
+                k = k_ref[:, cols].astype(f32)
+                v = v_ref[:, cols]
+                kg = grads[0, :, inner].astype(f32) + (dot(v, back, 1, 1) + norm) * slope(k)
+                kg_ref[:, cols] = kg.astype(bf16)
+                vg = grads[1, :, inner].astype(f32) + dot(feature(k).astype(bf16), back, 1, 0)
+                vg_ref[:, cols] = vg.astype(bf16)
 
 
 def key_value(z, keys, values, backs, firsts, seconds):
-    piece = pl.BlockSpec((2, SHARE, HALF), lambda i: (0, 0, 0))
-    whole = pl.BlockSpec((SHARE, 4 * GROUP), lambda i: (0, 0))
-    state = pl.BlockSpec((ROWS, DH), lambda i: (0, 0))
+    piece = pl.BlockSpec((2, SHARE, HALF), lambda i, z: (0, 0, 0))
+    group = pl.BlockSpec((SHARE, GROUP), lambda i, z: (0, lax.rem(z[0] + 4 - i, 4)))
+    state = pl.BlockSpec((ROWS, DH), lambda i, z: (0, 0))
     return pl.pallas_call(
         key_value_kernel,
-        grid=(1,),
+        grid_spec=pltpu.PrefetchScalarGridSpec(
+            num_scalar_prefetch=1,
+            grid=(4,),
+            in_specs=[group] * 2 + [state] * 4 + [piece] * 8,
+            out_specs=[group] * 2,
+        ),
         out_shape=[shape((SHARE, 4 * GROUP))] * 2,
-        in_specs=[SMEM] + [whole] * 2 + [state] * 4 + [piece] * 8,
-        out_specs=[whole] * 2,
-        compiler_params=params(),
+        compiler_params=params(24),
         cost_estimate=cost(5),
         name="key_value",
     )(z, keys, values, *backs, *firsts, *seconds)
@@ -496,18 +520,18 @@
     z = lax.axis_index("head").astype(jnp.int32).reshape(1)
     gates = jax.nn.sigmoid(gate_logits)
     arrays = (k, v, q, y)
-    partials, own, firsts, seconds = front(z, *arrays)
+    partials, own, first, queries_b, keys_b = front(z, *arrays)
     partials = to_peers(partials)
-    in_a = to_peers(firsts)
-    in_b = to_peers(seconds)
+    in_a = to_peers(first)
+    qy_b = to_peers(queries_b)
+    kv_b = to_peers(keys_b)
     slices = swap(update(own, partials))
     memory = swap(scan(slices, False))
-    local_a = attention(z, gates, arrays, in_a, 0)
-    grads, out_a = read_memory(z, gates, memory, q, y, in_a, 0, local=local_a)
+    local = attention(z, gates, arrays, in_a, 0)
+    grads, out_a = read_memory(z, gates, memory, q, y, in_a, qy_b, local)
     back_a = to_peers(out_a[1:])
-    grads, _ = read_memory(z, gates, memory, q, y, in_b, 1, earlier=grads)
     slices = swap(grads)
-    out_b = attention(z, gates, arrays, in_b, 1, [memory])
+    out_b = attention(z, gates, arrays, kv_b + qy_b, 1, [memory])
     back_b = to_peers(out_b[1:])
     state = compact(swap(scan(slices, True)))
     states = [state] + to_peers([state] * 3)

time: 161 us -> 140 us (0.87)
  waiting for transfers between devices: 36.6 us -> 24 us
  Pallas kernels: 52.5 us -> 41 us
  starting transfers between devices: 48.5 us -> 54.4 us
  local copies, waits for them, and re-layouts: 5.15 us -> 2.57 us
    ppermute x18 -> x21, waiting for transfers between devices: 31.6 us -> 20.2 us  [to_peers(): lax.ppermute(block, 'head', [(i, (i + shift) % 4) for i in range(4)])]
    ppermute x18 -> x21, starting transfers between devices: 29.7 us -> 36 us  [to_peers(): lax.ppermute(block, 'head', [(i, (i + shift) % 4) for i in range(4)])]
    pallas_call x3 -> x2, Pallas kernels: 15.8 us -> 10.5 us  [the longest x1 7.63 us: read_memory(): pl.pallas_call(memory_kernel, out_shape=[shape((32, 32, DH))] + [shape((4...]
    unnamed x42 -> x34, local copies, waits for them, and re-layouts: 5.15 us -> 2.57 us
  transfers between devices with their start and end apart: 21 -> 24, of which waited for: 9 -> 9; matrix products, arithmetic and copies ran while one was open for 0% -> 0% of each run, Pallas kernels for 19% -> 23%
where the time goes in v1:
time: 140 us
  starting transfers between devices  54.4 us (39%)
  Pallas kernels  41 us (29%)
  waiting for transfers between devices  24 us (17%)
  blocking collectives  16.1 us (12%)
  local copies, waits for them, and re-layouts  2.57 us (2%)
    ppermute x21, starting transfers between devices, to_peers(): lax.ppermute(block, 'head', [(i, (i + shift) % 4) for i in range(4)])  36 us
    pallas_call x2, Pallas kernels, attention(): pl.pallas_call(functools.partial(attention_kernel, half=half), out_shape=...  20.4 us
    ppermute x21, waiting for transfers between devices, to_peers(): lax.ppermute(block, 'head', [(i, (i + shift) % 4) for i in range(4)])  20.2 us
    all_to_all x3, starting transfers between devices, swap(): return lax.all_to_all(x, 'seq', 0, 0, tiled=True)  18.5 us
    all_to_all x1, blocking collectives, swap(): return lax.all_to_all(x, 'seq', 0, 0, tiled=True)  16.1 us
    pallas_call x1, Pallas kernels, read_memory(): pl.pallas_call(memory_kernel, out_shape=[shape((32, 32, DH))] + [shape((4...  7.63 us
    pallas_call x1, Pallas kernels, front(): pl.pallas_call(front_kernel, out_shape=[shape((ROWS, DH))] * 3 + [shape((...  5.74 us
    all_to_all x3, waiting for transfers between devices, swap(): return lax.all_to_all(x, 'seq', 0, 0, tiled=True)  3.79 us
  transfers between devices with their start and end apart: 24, of which 9 were waited for; matrix products, arithmetic and copies ran while one was open for 0% of the time, Pallas kernels for 23%

profile of v1, /device:TPU:0, one launch (start us, length us, event | category | flops | bytes accessed | tf_op | source)
XLA Modules:
  0.0 139.6 jit_solution(1074950806173596951)
XLA Ops:
  0.6 5.7 %front.1 = (bf16[576,128]{1,0:T(8,128)(2,1)}, bf16[576,128]{1,0:T(8,128)(2,1)}, bf16[576,128]{1,0:T(8,128)(2,1)}, f32[576,128]{1,0:T(8,128)}, bf16[4,256,256]{2,...) custom-call(s32[1]{0:T(128)} %bitcast.z_ref, ...), custom_call_target="tpu_custom_call" | custom-call | flops 3000000000 | bytes 12000000 | tf_op jit(solution)/shard_map/front/pallas_call | solution.py:117
  6.4 2.1 %collective-permute-start = (bf16[576,128]{1,0:T(8,128)(2,1)}, bf16[576,128]{1,0:T(8,128)(2,1)S(1)}, u32[]{:S(2)}, u32[]{:S(2)}) collective-permute-start(bf16[576,128]{1,0:T(8,128)(2,1)} %get-tuple-element.34), channel_id=1, source_target_pairs={{0,1},{1,2},{2,3},{3,0},{4,5},{5,6},{6,7},{7,4},{8,9},{9,10},{10,1... | collective-permute-start | bytes 442376 | tf_op jit(solution)/shard_map/ppermute | solution.py:511
  8.5 3.6 %collective-permute-start.1 = (bf16[576,128]{1,0:T(8,128)(2,1)}, bf16[576,128]{1,0:T(8,128)(2,1)S(1)}, u32[]{:S(2)}, u32[]{:S(2)}) collective-permute-start(bf16[576,128]{1,0:T(8,128)(2,1)} %get-tuple-element.35), channel_id=1, source_target_pairs={{0,2},{1,3},{2,0},{3,1},{4,6},{5,7},{6,4},{7,5},{8,10},{9,11},{10,... | collective-permute-start | bytes 442376 | tf_op jit(solution)/shard_map/ppermute | solution.py:511
  12.1 1.0 collective-permute-start.2
  13.1 1.0 collective-permute-start.3
  14.7 2.9 %collective-permute-start.5 = (bf16[4,256,256]{2,1,0:T(8,128)(2,1)}, bf16[4,256,256]{2,1,0:T(8,128)(2,1)S(1)}, u32[]{:S(2)}, u32[]{:S(2)}) collective-permute-start(bf16[4,256,256]{2,1,0:T(8,128)(2,1)} %get-tuple-element.39), channel_id=1, source_target_pairs={{0,3},{1,0},{2,1},{3,2},{4,7},{5,4},{6,5},{7,6},{8,11},{9,8},{10,9... | collective-permute-start | bytes 1572872 | tf_op jit(solution)/shard_map/ppermute | solution.py:511
  17.5 2.6 %collective-permute-done.1.r2 = bf16[576,128]{1,0:T(8,128)(2,1)S(1)} collective-permute-done((bf16[576,128]{1,0:T(8,128)(2,1)}, bf16[576,128]{1,0:T(8,128)(2,1)S(1)}, u32[]{:S(2)}, u32[]{:S(2)}) %collective-permute-start.1) | collective-permute-done | bytes 147488 | tf_op jit(solution)/shard_map/ppermute | solution.py:511
  20.1 8.2 %collective-permute-done.2.r3 = bf16[576,128]{1,0:T(8,128)(2,1)S(1)} collective-permute-done((bf16[576,128]{1,0:T(8,128)(2,1)}, bf16[576,128]{1,0:T(8,128)(2,1)S(1)}, u32[]{:S(2)}, u32[]{:S(2)}) %collective-permute-start.2) | collective-permute-done | bytes 147488 | tf_op jit(solution)/shard_map/ppermute | solution.py:511
  28.4 1.0 copy-done.4
  30.1 7.3 %all-to-all-start = ((f32[32,24,128]{2,1,0:T(8,128)}), f32[32,24,128]{2,1,0:T(8,128)S(1)}, u32[]{:S(2)}, u32[]{:S(2)}) async-start(f32[32,24,128]{2,1,0:T(8,128)} %update.1), calls=%async_computation | async-start | bytes 786432 | tf_op jit(solution)/shard_map/all_to_all | solution.py:516
  37.5 2.3 %collective-permute-start.6 = (bf16[2,256,256]{2,1,0:T(8,128)(2,1)}, bf16[2,256,256]{2,1,0:T(8,128)(2,1)S(1)}, u32[]{:S(2)}, u32[]{:S(2)}) collective-permute-start(bf16[2,256,256]{2,1,0:T(8,128)(2,1)} %get-tuple-element.40), channel_id=1, source_target_pairs={{0,1},{1,2},{2,3},{3,0},{4,5},{5,6},{6,7},{7,4},{8,9},{9,10},{10,1... | collective-permute-start | bytes 786440 | tf_op jit(solution)/shard_map/ppermute | solution.py:511
  39.8 3.3 %collective-permute-start.7 = (bf16[2,256,256]{2,1,0:T(8,128)(2,1)}, bf16[2,256,256]{2,1,0:T(8,128)(2,1)S(1)}, u32[]{:S(2)}, u32[]{:S(2)}) collective-permute-start(bf16[2,256,256]{2,1,0:T(8,128)(2,1)} %get-tuple-element.41), channel_id=1, source_target_pairs={{0,2},{1,3},{2,0},{3,1},{4,6},{5,7},{6,4},{7,5},{8,10},{9,11},{10,... | collective-permute-start | bytes 786440 | tf_op jit(solution)/shard_map/ppermute | solution.py:511
  43.6 3.8 %all-to-all-done.in_ref = f32[32,24,128]{2,1,0:T(8,128)S(1)} async-done(((f32[32,24,128]{2,1,0:T(8,128)}), f32[32,24,128]{2,1,0:T(8,128)S(1)}, u32[]{:S(2)}, u32[]{:S(2)}) %all-to-all-start) | async-done | bytes 393248 | tf_op jit(solution)/shard_map/all_to_all | solution.py:516
  47.4 1.3 scan_earlier.1
  48.8 4.0 %all-to-all-start.1 = ((f32[32,24,128]{2,1,0:T(8,128)}), f32[32,24,128]{2,1,0:T(8,128)S(1)}, u32[]{:S(2)}, u32[]{:S(2)}) async-start(f32[32,24,128]{2,1,0:T(8,128)} %scan_earlier.1), calls=%async_computation.1 | async-start | bytes 786432 | tf_op jit(solution)/shard_map/all_to_all | solution.py:516
  52.8 4.1 %collective-permute-start.8 = (bf16[2,256,256]{2,1,0:T(8,128)(2,1)S(1)}, bf16[2,256,256]{2,1,0:T(8,128)(2,1)}, u32[]{:S(2)}, u32[]{:S(2)}) collective-permute-start(bf16[2,256,256]{2,1,0:T(8,128)(2,1)S(1)} %copy-done.13), channel_id=1, source_target_pairs={{0,3},{1,0},{2,1},{3,2},{4,7},{5,4},{6,5},{7,6},{8,11},{9,8},{10,9... | collective-permute-start | bytes 786440 | tf_op jit(solution)/shard_map/ppermute | solution.py:511
  57.1 1.5 %collective-permute-start.13 = (bf16[2,256,256]{2,1,0:T(8,128)(2,1)S(1)}, bf16[2,256,256]{2,1,0:T(8,128)(2,1)}, u32[]{:S(2)}, u32[]{:S(2)}) collective-permute-start(bf16[2,256,256]{2,1,0:T(8,128)(2,1)S(1)} %copy-done.10), channel_id=1, source_target_pairs={{0,2},{1,3},{2,0},{3,1},{4,6},{5,7},{6,4},{7,5},{8,10},{9,11},{10,... | collective-permute-start | bytes 786440 | tf_op jit(solution)/shard_map/ppermute | solution.py:511
  58.7 9.5 %shard_map.84 = (f32[1024,256]{1,0:T(8,128)}, f32[1024,256]{1,0:T(8,128)}, bf16[2,1024,256]{2,1,0:T(8,128)(2,1)}) custom-call(s32[1]{0:T(128)} %bitcast.z_ref, f32[4]{0:T(128)} %add_divide_fusion.g_ref, bf16[256,2048]{1,0:T(8,128)(2,1)} %k_ref.7, bf16[256,2048]{1,0:T(8,128)(2,1)} %v_ref.7, bf16[256,2048]{1,0:T(8,128)(2,1)} %q_ref.7, ...), custom_call_target="tpu_custom_call" | custom-call | flops 5000000000 | bytes 20000000 | tf_op jit(solution)/shard_map/pallas_call | solution.py:328
  68.2 2.5 %collective-permute-start.14 = (bf16[2,256,256]{2,1,0:T(8,128)(2,1)S(1)}, bf16[2,256,256]{2,1,0:T(8,128)(2,1)S(1)}, u32[]{:S(2)}, u32[]{:S(2)}) collective-permute-start(bf16[2,256,256]{2,1,0:T(8,128)(2,1)S(1)} %copy-done.9), channel_id=1, source_target_pairs={{0,3},{1,0},{2,1},{3,2},{4,7},{5,4},{6,5},{7,6},{8,11},{9,8},{10,9... | collective-permute-start | bytes 786440 | tf_op jit(solution)/shard_map/ppermute | solution.py:511
  71.7 7.6 %read_memory.1 = (bf16[32,32,128]{2,1,0:T(8,128)(2,1)}, bf16[4,256,256]{2,1,0:T(8,128)(2,1)}, bf16[4,256,256]{2,1,0:T(8,128)(2,1)}, bf16[4,256,256]{2,1,0:T(8,128)(2,1)}, bf16[4,256,256]{2,1,0:T(8,128)(2,1)}) custom-call(s32[1]{0:T(128)} %bitcast.z_ref, f32[4]{0:T(128)} %add_divide_fusion.g_ref, f32[32,24,128]{2,1,0:T(8,128)} %copy-done.5, ...), custom_call_target="tpu_custom_call" | custom-call | flops 4000000000 | bytes 16000000 | tf_op jit(solution)/shard_map/read_memory/pallas_call | solution.py:406
  79.5 2.9 %collective-permute-start.10 = (bf16[4,256,256]{2,1,0:T(8,128)(2,1)}, bf16[4,256,256]{2,1,0:T(8,128)(2,1)S(1)}, u32[]{:S(2)}, u32[]{:S(2)}) collective-permute-start(bf16[4,256,256]{2,1,0:T(8,128)(2,1)} %get-tuple-element.48), channel_id=1, source_target_pairs={{0,2},{1,3},{2,0},{3,1},{4,6},{5,7},{6,4},{7,5},{8,10},{9,11},{10,... | collective-permute-start | bytes 1572872 | tf_op jit(solution)/shard_map/ppermute | solution.py:511
  82.4 7.1 %all-to-all-start.2 = ((bf16[32,32,128]{2,1,0:T(8,128)(2,1)}), bf16[32,32,128]{2,1,0:T(8,128)(2,1)S(1)}, u32[]{:S(2)}, u32[]{:S(2)}) async-start(bf16[32,32,128]{2,1,0:T(8,128)(2,1)} %get-tuple-element.59), calls=%async_computation.2 | async-start | bytes 524288 | tf_op jit(solution)/shard_map/all_to_all | solution.py:516
  89.6 2.1 %collective-permute-start.11 = (bf16[4,256,256]{2,1,0:T(8,128)(2,1)}, bf16[4,256,256]{2,1,0:T(8,128)(2,1)S(1)}, u32[]{:S(2)}, u32[]{:S(2)}) collective-permute-start(bf16[4,256,256]{2,1,0:T(8,128)(2,1)} %get-tuple-element.49), channel_id=1, source_target_pairs={{0,3},{1,0},{2,1},{3,2},{4,7},{5,4},{6,5},{7,6},{8,11},{9,8},{10,9... | collective-permute-start | bytes 1572872 | tf_op jit(solution)/shard_map/ppermute | solution.py:511
  92.4 10.9 %shard_map.85 = (bf16[4,256,256]{2,1,0:T(8,128)(2,1)}, bf16[4,256,256]{2,1,0:T(8,128)(2,1)}, bf16[4,256,256]{2,1,0:T(8,128)(2,1)}, bf16[4,256,256]{2,1,0:T(8,128)(2,1)}) custom-call(s32[1]{0:T(128)} %bitcast.z_ref, f32[4]{0:T(128)} %add_divide_fusion.g_ref, bf16[256,2048]{1,0:T(8,128)(2,1)} %k_ref.7, bf16[256,2048]{1,0:T(8,128)(2,1)} %v_ref.7, ...), custom_call_target="tpu_custom_call" | custom-call | flops 6000000000 | bytes 24000000 | tf_op jit(solution)/shard_map/pallas_call | solution.py:328
  103.3 1.5 %collective-permute-start.16 = (bf16[4,256,256]{2,1,0:T(8,128)(2,1)}, bf16[4,256,256]{2,1,0:T(8,128)(2,1)S(1)}, u32[]{:S(2)}, u32[]{:S(2)}) collective-permute-start(bf16[4,256,256]{2,1,0:T(8,128)(2,1)} %get-tuple-element.55), channel_id=1, source_target_pairs={{0,2},{1,3},{2,0},{3,1},{4,6},{5,7},{6,4},{7,5},{8,10},{9,11},{10,... | collective-permute-start | bytes 1572872 | tf_op jit(solution)/shard_map/ppermute | solution.py:511
  105.4 1.9 %collective-permute-start.17 = (bf16[4,256,256]{2,1,0:T(8,128)(2,1)}, bf16[4,256,256]{2,1,0:T(8,128)(2,1)S(1)}, u32[]{:S(2)}, u32[]{:S(2)}) collective-permute-start(bf16[4,256,256]{2,1,0:T(8,128)(2,1)} %get-tuple-element.56), channel_id=1, source_target_pairs={{0,3},{1,0},{2,1},{3,2},{4,7},{5,4},{6,5},{7,6},{8,11},{9,8},{10,9... | collective-permute-start | bytes 1572872 | tf_op jit(solution)/shard_map/ppermute | solution.py:511
  108.1 16.1 %all_to_all.20.in_ref = bf16[32,32,128]{2,1,0:T(8,128)(2,1)S(1)} all-to-all(bf16[32,32,128]{2,1,0:T(8,128)(2,1)S(1)} %scan_later.1), channel_id=1, replica_groups=mesh['seq'=32,'head'=4] {'seq'}, dimensions={0} | all-to-all | bytes 524288 | tf_op jit(solution)/shard_map/all_to_all | solution.py:516
  124.4 2.1 %collective-permute-start.19 = (bf16[576,128]{1,0:T(8,128)(2,1)S(1)}, bf16[576,128]{1,0:T(8,128)(2,1)S(1)}, u32[]{:S(2)}, u32[]{:S(2)}) collective-permute-start(bf16[576,128]{1,0:T(8,128)(2,1)S(1)} %compact.1.rest_0_), channel_id=1, source_target_pairs={{0,2},{1,3},{2,0},{3,1},{4,6},{5,7},{6,4},{7,5},{8,10},{9,11},{10,... | collective-permute-start | bytes 442376 | tf_op jit(solution)/shard_map/ppermute | solution.py:511
  126.6 4.2 %collective-permute-done.15.rest_5_.rest_9_ = bf16[4,256,256]{2,1,0:T(8,128)(2,1)S(1)} collective-permute-done((bf16[4,256,256]{2,1,0:T(8,128)(2,1)}, bf16[4,256,256]{2,1,0:T(8,128)(2,1)S(1)}, u32[]{:S(2)}, u32[]{:S(2)}) %collective-permute-start.15) | collective-permute-done | bytes 524320 | tf_op jit(solution)/shard_map/ppermute | solution.py:511
  131.7 1.5 %results.1 = (bf16[256,2048]{1,0:T(8,128)(2,1)}, bf16[256,2048]{1,0:T(8,128)(2,1)}) custom-call(s32[1]{0:T(128)} %bitcast.z_ref, bf16[4,256,256]{2,1,0:T(8,128)(2,1)S(1)} %copy-done.2, bf16[4,256,256]{2,1,0:T(8,128)(2,1)S(1)} %collective-permute-done.9.rest_1_.rest_5_, bf16[4,256,256]{2,1,0:T(8,128)(2,1)S(1)} %collective-permute-done.10.rest_2_.rest_6_, ...), custom_call_target="tpu_custom_call" | custom-call | flops 1500000000 | bytes 6000000 | tf_op jit(solution)/shard_map/results/pallas_call | solution.py:438
  133.2 3.0 %collective-permute-done.18.rest_1_ = bf16[576,128]{1,0:T(8,128)(2,1)S(1)} collective-permute-done((bf16[576,128]{1,0:T(8,128)(2,1)S(1)}, bf16[576,128]{1,0:T(8,128)(2,1)S(1)}, u32[]{:S(2)}, u32[]{:S(2)}) %collective-permute-start.18) | collective-permute-done | bytes 147488 | tf_op jit(solution)/shard_map/ppermute | solution.py:511
  136.7 2.9 %key_value.1 = (bf16[256,2048]{1,0:T(8,128)(2,1)}, bf16[256,2048]{1,0:T(8,128)(2,1)}) custom-call(s32[1]{0:T(128)} %bitcast.z_ref, bf16[256,2048]{1,0:T(8,128)(2,1)S(1)} %copy-done, bf16[256,2048]{1,0:T(8,128)(2,1)S(1)} %copy-done.1, bf16[576,128]{1,0:T(8,128)(2,1)S(1)} %compact.1.rest_0_, bf16[576,128]{1,0:T(8,128)(2,1)S(1)} %collective-permute-done.18.rest_1_, ...), custom_call_target="tpu_custom_call" | custom-call | flops 2500000000 | bytes 10000000 | tf_op jit(solution)/shard_map/key_value/pallas_call | solution.py:493
  (62 shorter events, 7.1 us)
Async XLA Ops:
  6.4 8.3 %collective-permute-start = (bf16[576,128]{1,0:T(8,128)(2,1)}, bf16[576,128]{1,0:T(8,128)(2,1)S(1)}, u32[]{:S(2)}, u32[]{:S(2)}) collective-permute-start(bf16[576,128]{1,0:T(8,128)(2,1)} %get-tuple-element.34), channel_id=1, source_target_pairs={{0,1},{1,2},{2,3},{3,0},{4,5},{5,6},{6,7},{7,4},{8,9},{9,10},{10,1... | collective-permute-start | bytes 442376 | tf_op jit(solution)/shard_map/ppermute | solution.py:511
  8.5 11.6 %collective-permute-start.1 = (bf16[576,128]{1,0:T(8,128)(2,1)}, bf16[576,128]{1,0:T(8,128)(2,1)S(1)}, u32[]{:S(2)}, u32[]{:S(2)}) collective-permute-start(bf16[576,128]{1,0:T(8,128)(2,1)} %get-tuple-element.35), channel_id=1, source_target_pairs={{0,2},{1,3},{2,0},{3,1},{4,6},{5,7},{6,4},{7,5},{8,10},{9,11},{10,... | collective-permute-start | bytes 442376 | tf_op jit(solution)/shard_map/ppermute | solution.py:511
  12.1 16.3 %collective-permute-start.2 = (bf16[576,128]{1,0:T(8,128)(2,1)}, bf16[576,128]{1,0:T(8,128)(2,1)S(1)}, u32[]{:S(2)}, u32[]{:S(2)}) collective-permute-start(bf16[576,128]{1,0:T(8,128)(2,1)} %get-tuple-element.36), channel_id=1, source_target_pairs={{0,3},{1,0},{2,1},{3,2},{4,7},{5,4},{6,5},{7,6},{8,11},{9,8},{10,9... | collective-permute-start | bytes 442376 | tf_op jit(solution)/shard_map/ppermute | solution.py:511
  13.1 39.7 %collective-permute-start.3 = (bf16[4,256,256]{2,1,0:T(8,128)(2,1)}, bf16[4,256,256]{2,1,0:T(8,128)(2,1)S(1)}, u32[]{:S(2)}, u32[]{:S(2)}) collective-permute-start(bf16[4,256,256]{2,1,0:T(8,128)(2,1)} %get-tuple-element.37), channel_id=1, source_target_pairs={{0,1},{1,2},{2,3},{3,0},{4,5},{5,6},{6,7},{7,4},{8,9},{9,10},{10,1... | collective-permute-start | bytes 1572872 | tf_op jit(solution)/shard_map/ppermute | solution.py:511
  14.1 42.9 %collective-permute-start.4 = (bf16[4,256,256]{2,1,0:T(8,128)(2,1)}, bf16[4,256,256]{2,1,0:T(8,128)(2,1)S(1)}, u32[]{:S(2)}, u32[]{:S(2)}) collective-permute-start(bf16[4,256,256]{2,1,0:T(8,128)(2,1)} %get-tuple-element.38), channel_id=1, source_target_pairs={{0,2},{1,3},{2,0},{3,1},{4,6},{5,7},{6,4},{7,5},{8,10},{9,11},{10,... | collective-permute-start | bytes 1572872 | tf_op jit(solution)/shard_map/ppermute | solution.py:511
  14.7 42.4 %collective-permute-start.5 = (bf16[4,256,256]{2,1,0:T(8,128)(2,1)}, bf16[4,256,256]{2,1,0:T(8,128)(2,1)S(1)}, u32[]{:S(2)}, u32[]{:S(2)}) collective-permute-start(bf16[4,256,256]{2,1,0:T(8,128)(2,1)} %get-tuple-element.39), channel_id=1, source_target_pairs={{0,3},{1,0},{2,1},{3,2},{4,7},{5,4},{6,5},{7,6},{8,11},{9,8},{10,9... | collective-permute-start | bytes 1572872 | tf_op jit(solution)/shard_map/ppermute | solution.py:511
  30.1 17.3 %all-to-all-start = ((f32[32,24,128]{2,1,0:T(8,128)}), f32[32,24,128]{2,1,0:T(8,128)S(1)}, u32[]{:S(2)}, u32[]{:S(2)}) async-start(f32[32,24,128]{2,1,0:T(8,128)} %update.1), calls=%async_computation | async-start | bytes 786432 | tf_op jit(solution)/shard_map/all_to_all | solution.py:516
  37.5 5.6 %copy-start.16 = (f32[4]{0:T(128)S(1)}, f32[4]{0:T(128)}, u32[]{:S(2)}) copy-start(f32[4]{0:T(128)} %param.8) | copy-start | bytes 52
  37.5 30.7 %collective-permute-start.6 = (bf16[2,256,256]{2,1,0:T(8,128)(2,1)}, bf16[2,256,256]{2,1,0:T(8,128)(2,1)S(1)}, u32[]{:S(2)}, u32[]{:S(2)}) collective-permute-start(bf16[2,256,256]{2,1,0:T(8,128)(2,1)} %get-tuple-element.40), channel_id=1, source_target_pairs={{0,1},{1,2},{2,3},{3,0},{4,5},{5,6},{6,7},{7,4},{8,9},{9,10},{10,1... | collective-permute-start | bytes 786440 | tf_op jit(solution)/shard_map/ppermute | solution.py:511
  39.8 31.0 %collective-permute-start.7 = (bf16[2,256,256]{2,1,0:T(8,128)(2,1)}, bf16[2,256,256]{2,1,0:T(8,128)(2,1)S(1)}, u32[]{:S(2)}, u32[]{:S(2)}) collective-permute-start(bf16[2,256,256]{2,1,0:T(8,128)(2,1)} %get-tuple-element.41), channel_id=1, source_target_pairs={{0,2},{1,3},{2,0},{3,1},{4,6},{5,7},{6,4},{7,5},{8,10},{9,11},{10,... | collective-permute-start | bytes 786440 | tf_op jit(solution)/shard_map/ppermute | solution.py:511
  48.7 8.2 %copy-start.11 = (bf16[2,256,256]{2,1,0:T(8,128)(2,1)S(1)}, bf16[2,256,256]{2,1,0:T(8,128)(2,1)}, u32[]{:S(2)}) copy-start(bf16[2,256,256]{2,1,0:T(8,128)(2,1)} %get-tuple-element.50) | copy-start | bytes 786436
  48.8 8.3 %copy-start.10 = (bf16[2,256,256]{2,1,0:T(8,128)(2,1)S(1)}, bf16[2,256,256]{2,1,0:T(8,128)(2,1)}, u32[]{:S(2)}) copy-start(bf16[2,256,256]{2,1,0:T(8,128)(2,1)} %get-tuple-element.51) | copy-start | bytes 786436
  48.8 22.0 %all-to-all-start.1 = ((f32[32,24,128]{2,1,0:T(8,128)}), f32[32,24,128]{2,1,0:T(8,128)S(1)}, u32[]{:S(2)}, u32[]{:S(2)}) async-start(f32[32,24,128]{2,1,0:T(8,128)} %scan_earlier.1), calls=%async_computation.1 | async-start | bytes 786432 | tf_op jit(solution)/shard_map/all_to_all | solution.py:516
  52.8 5.8 %copy-start.6 = (bf16[4,256,256]{2,1,0:T(8,128)(2,1)}, bf16[4,256,256]{2,1,0:T(8,128)(2,1)S(1)}, u32[]{:S(2)}) copy-start(bf16[4,256,256]{2,1,0:T(8,128)(2,1)S(1)} %collective-permute-done.3.refs_0_.a1) | copy-start | bytes 1572868
  52.8 18.0 %collective-permute-start.8 = (bf16[2,256,256]{2,1,0:T(8,128)(2,1)S(1)}, bf16[2,256,256]{2,1,0:T(8,128)(2,1)}, u32[]{:S(2)}, u32[]{:S(2)}) collective-permute-start(bf16[2,256,256]{2,1,0:T(8,128)(2,1)S(1)} %copy-done.13), channel_id=1, source_target_pairs={{0,3},{1,0},{2,1},{3,2},{4,7},{5,4},{6,5},{7,6},{8,11},{9,8},{10,9... | collective-permute-start | bytes 786440 | tf_op jit(solution)/shard_map/ppermute | solution.py:511
  57.0 32.6 %collective-permute-start.12 = (bf16[2,256,256]{2,1,0:T(8,128)(2,1)S(1)}, bf16[2,256,256]{2,1,0:T(8,128)(2,1)}, u32[]{:S(2)}, u32[]{:S(2)}) collective-permute-start(bf16[2,256,256]{2,1,0:T(8,128)(2,1)S(1)} %copy-done.11), channel_id=1, source_target_pairs={{0,1},{1,2},{2,3},{3,0},{4,5},{5,6},{6,7},{7,4},{8,9},{9,10},{10,1... | collective-permute-start | bytes 786440 | tf_op jit(solution)/shard_map/ppermute | solution.py:511
  57.1 11.1 %copy-start.9 = (bf16[2,256,256]{2,1,0:T(8,128)(2,1)S(1)}, bf16[2,256,256]{2,1,0:T(8,128)(2,1)}, u32[]{:S(2)}) copy-start(bf16[2,256,256]{2,1,0:T(8,128)(2,1)} %get-tuple-element.52) | copy-start | bytes 786436
  57.1 34.6 %collective-permute-start.13 = (bf16[2,256,256]{2,1,0:T(8,128)(2,1)S(1)}, bf16[2,256,256]{2,1,0:T(8,128)(2,1)}, u32[]{:S(2)}, u32[]{:S(2)}) collective-permute-start(bf16[2,256,256]{2,1,0:T(8,128)(2,1)S(1)} %copy-done.10), channel_id=1, source_target_pairs={{0,2},{1,3},{2,0},{3,1},{4,6},{5,7},{6,4},{7,5},{8,10},{9,11},{10,... | collective-permute-start | bytes 786440 | tf_op jit(solution)/shard_map/ppermute | solution.py:511
  68.2 23.4 %collective-permute-start.14 = (bf16[2,256,256]{2,1,0:T(8,128)(2,1)S(1)}, bf16[2,256,256]{2,1,0:T(8,128)(2,1)S(1)}, u32[]{:S(2)}, u32[]{:S(2)}) collective-permute-start(bf16[2,256,256]{2,1,0:T(8,128)(2,1)S(1)} %copy-done.9), channel_id=1, source_target_pairs={{0,3},{1,0},{2,1},{3,2},{4,7},{5,4},{6,5},{7,6},{8,11},{9,8},{10,9... | collective-permute-start | bytes 786440 | tf_op jit(solution)/shard_map/ppermute | solution.py:511
  79.3 26.1 %collective-permute-start.9 = (bf16[4,256,256]{2,1,0:T(8,128)(2,1)}, bf16[4,256,256]{2,1,0:T(8,128)(2,1)S(1)}, u32[]{:S(2)}, u32[]{:S(2)}) collective-permute-start(bf16[4,256,256]{2,1,0:T(8,128)(2,1)} %get-tuple-element.47), channel_id=1, source_target_pairs={{0,1},{1,2},{2,3},{3,0},{4,5},{5,6},{6,7},{7,4},{8,9},{9,10},{10,1... | collective-permute-start | bytes 1572872 | tf_op jit(solution)/shard_map/ppermute | solution.py:511
  79.5 44.7 %collective-permute-start.10 = (bf16[4,256,256]{2,1,0:T(8,128)(2,1)}, bf16[4,256,256]{2,1,0:T(8,128)(2,1)S(1)}, u32[]{:S(2)}, u32[]{:S(2)}) collective-permute-start(bf16[4,256,256]{2,1,0:T(8,128)(2,1)} %get-tuple-element.48), channel_id=1, source_target_pairs={{0,2},{1,3},{2,0},{3,1},{4,6},{5,7},{6,4},{7,5},{8,10},{9,11},{10,... | collective-permute-start | bytes 1572872 | tf_op jit(solution)/shard_map/ppermute | solution.py:511
  82.4 24.9 %all-to-all-start.2 = ((bf16[32,32,128]{2,1,0:T(8,128)(2,1)}), bf16[32,32,128]{2,1,0:T(8,128)(2,1)S(1)}, u32[]{:S(2)}, u32[]{:S(2)}) async-start(bf16[32,32,128]{2,1,0:T(8,128)(2,1)} %get-tuple-element.59), calls=%async_computation.2 | async-start | bytes 524288 | tf_op jit(solution)/shard_map/all_to_all | solution.py:516
  89.6 34.9 %collective-permute-start.11 = (bf16[4,256,256]{2,1,0:T(8,128)(2,1)}, bf16[4,256,256]{2,1,0:T(8,128)(2,1)S(1)}, u32[]{:S(2)}, u32[]{:S(2)}) collective-permute-start(bf16[4,256,256]{2,1,0:T(8,128)(2,1)} %get-tuple-element.49), channel_id=1, source_target_pairs={{0,3},{1,0},{2,1},{3,2},{4,7},{5,4},{6,5},{7,6},{8,11},{9,8},{10,9... | collective-permute-start | bytes 1572872 | tf_op jit(solution)/shard_map/ppermute | solution.py:511
  103.2 27.5 %collective-permute-start.15 = (bf16[4,256,256]{2,1,0:T(8,128)(2,1)}, bf16[4,256,256]{2,1,0:T(8,128)(2,1)S(1)}, u32[]{:S(2)}, u32[]{:S(2)}) collective-permute-start(bf16[4,256,256]{2,1,0:T(8,128)(2,1)} %get-tuple-element.54), channel_id=1, source_target_pairs={{0,1},{1,2},{2,3},{3,0},{4,5},{5,6},{6,7},{7,4},{8,9},{9,10},{10,1... | collective-permute-start | bytes 1572872 | tf_op jit(solution)/shard_map/ppermute | solution.py:511
  103.3 27.4 %collective-permute-start.16 = (bf16[4,256,256]{2,1,0:T(8,128)(2,1)}, bf16[4,256,256]{2,1,0:T(8,128)(2,1)S(1)}, u32[]{:S(2)}, u32[]{:S(2)}) collective-permute-start(bf16[4,256,256]{2,1,0:T(8,128)(2,1)} %get-tuple-element.55), channel_id=1, source_target_pairs={{0,2},{1,3},{2,0},{3,1},{4,6},{5,7},{6,4},{7,5},{8,10},{9,11},{10,... | collective-permute-start | bytes 1572872 | tf_op jit(solution)/shard_map/ppermute | solution.py:511
  105.4 26.3 %collective-permute-start.17 = (bf16[4,256,256]{2,1,0:T(8,128)(2,1)}, bf16[4,256,256]{2,1,0:T(8,128)(2,1)S(1)}, u32[]{:S(2)}, u32[]{:S(2)}) collective-permute-start(bf16[4,256,256]{2,1,0:T(8,128)(2,1)} %get-tuple-element.56), channel_id=1, source_target_pairs={{0,3},{1,0},{2,1},{3,2},{4,7},{5,4},{6,5},{7,6},{8,11},{9,8},{10,9... | collective-permute-start | bytes 1572872 | tf_op jit(solution)/shard_map/ppermute | solution.py:511
  124.2 7.5 %copy-start.2 = (bf16[4,256,256]{2,1,0:T(8,128)(2,1)S(1)}, bf16[4,256,256]{2,1,0:T(8,128)(2,1)}, u32[]{:S(2)}) copy-start(bf16[4,256,256]{2,1,0:T(8,128)(2,1)} %get-tuple-element.46.rest_0_.rest_4_) | copy-start | bytes 1572868
  124.2 7.5 %copy-start.3 = (bf16[4,256,256]{2,1,0:T(8,128)(2,1)S(1)}, bf16[4,256,256]{2,1,0:T(8,128)(2,1)}, u32[]{:S(2)}) copy-start(bf16[4,256,256]{2,1,0:T(8,128)(2,1)} %get-tuple-element.53.rest_4_.rest_8_) | copy-start | bytes 1572868
  124.2 11.9 %collective-permute-start.18 = (bf16[576,128]{1,0:T(8,128)(2,1)S(1)}, bf16[576,128]{1,0:T(8,128)(2,1)S(1)}, u32[]{:S(2)}, u32[]{:S(2)}) collective-permute-start(bf16[576,128]{1,0:T(8,128)(2,1)S(1)} %compact.1.rest_0_), channel_id=1, source_target_pairs={{0,1},{1,2},{2,3},{3,0},{4,5},{5,6},{6,7},{7,4},{8,9},{9,10},{10,1... | collective-permute-start | bytes 442376 | tf_op jit(solution)/shard_map/ppermute | solution.py:511
  124.4 11.7 %collective-permute-start.19 = (bf16[576,128]{1,0:T(8,128)(2,1)S(1)}, bf16[576,128]{1,0:T(8,128)(2,1)S(1)}, u32[]{:S(2)}, u32[]{:S(2)}) collective-permute-start(bf16[576,128]{1,0:T(8,128)(2,1)S(1)} %compact.1.rest_0_), channel_id=1, source_target_pairs={{0,2},{1,3},{2,0},{3,1},{4,6},{5,7},{6,4},{7,5},{8,10},{9,11},{10,... | collective-permute-start | bytes 442376 | tf_op jit(solution)/shard_map/ppermute | solution.py:511
  130.8 6.0 %collective-permute-start.20 = (bf16[576,128]{1,0:T(8,128)(2,1)S(1)}, bf16[576,128]{1,0:T(8,128)(2,1)S(1)}, u32[]{:S(2)}, u32[]{:S(2)}) collective-permute-start(bf16[576,128]{1,0:T(8,128)(2,1)S(1)} %compact.1.rest_0_), channel_id=1, source_target_pairs={{0,3},{1,0},{2,1},{3,2},{4,7},{5,4},{6,5},{7,6},{8,11},{9,8},{10,9... | collective-permute-start | bytes 442376 | tf_op jit(solution)/shard_map/ppermute | solution.py:511
  131.7 5.1 %copy-start.1 = (bf16[256,2048]{1,0:T(8,128)(2,1)S(1)}, bf16[256,2048]{1,0:T(8,128)(2,1)}, u32[]{:S(2)}) copy-start(bf16[256,2048]{1,0:T(8,128)(2,1)} %v_ref.7) | copy-start | bytes 3145732
  (9 other events, 18.2 us)
